TPU v7x, 512 devices: a whole 4x8x8 slice. The times are simulated.
512 devices in a mesh: samp: 8 (over z), pair: 16 (over y_lo, x), recv: 4 (over y_hi, core).
Axes of the slice: x: 4, y: 8 (y_hi: 2, y_lo: 4; y = y_hi * 4 + y_lo), z: 8, core: 2. Of those that a mesh axis runs over, the one named last changes fastest.
Arguments:
- cell_expression: bfloat16 [32, 16384, 2048], P('samp', 'recv', 'pair'), may hold values from 0 to 24
- cell_labels: int32 [32, 16384], P('samp', 'recv'), may hold values from 0 to 127, as said below
- ligand_gene: int32 [2048], P('pair'), may hold values from 0 to 2047
- receptor_gene: int32 [2048], P('pair'), may hold values from 0 to 2047
- pair_factor: bfloat16 [2048, 32], P('pair'), may hold values from -0.53033009 to 0.53033009
- sender_factor: bfloat16 [128, 32], replicated, may hold values from -0.5 to 0.5
- receiver_factor: bfloat16 [128, 32], P('recv'), may hold values from -2.5 to 2.5
Outputs:
- sample_factor: float32 [32, 32], P('samp')
Inputs may be any that keep to these rules, and one draw needn't show every extreme that they name: `cell_labels`: in every sample one cell type has no cell.
All inputs are finite; a program needn't handle non-finite values.
Results may differ from a plain program's by a relative error of at most 0.0051.
Values may be sent and summed in bfloat16 or wider, within the bound.
No kernel may reach another device: no remote copies, remote signals or barrier semaphores. Data moves between devices by JAX's collectives and lax.ppermute only.
A program may use at most 64 MiB of HBM per device.

v0:
```python
import jax
import jax.numpy as jnp
from jax import lax
from jax.sharding import PartitionSpec as P


def body(
    cell_expression,
    cell_labels,
    ligand_gene,
    receptor_gene,
    pair_factor,
    sender_factor,
    receiver_factor,
):
    clusters = sender_factor.shape[0]
    factor_rank = sender_factor.shape[1]
    block_width = receiver_factor.shape[0]
    member = (
        cell_labels[:, :, None] == jnp.arange(clusters, dtype=jnp.int32)[None, None, :]
    ).astype(jnp.bfloat16)
    part_sums = jnp.einsum(
        "scg,sck->sgk", cell_expression, member, preferred_element_type=jnp.float32
    )
    part_counts = jnp.sum(member, axis=1, dtype=jnp.float32)
    receiver_start = lax.axis_index("recv") * block_width
    cluster_total, cell_count = lax.psum((part_sums, part_counts), "recv")
    cluster_mean = (cluster_total / jnp.maximum(cell_count, 1.0)[:, None, :]).astype(jnp.bfloat16)
    segment = lax.all_gather(cluster_mean, "pair", axis=1, tiled=True)
    ligand_table = jnp.einsum(
        "sga,ar->srg", segment, sender_factor, preferred_element_type=jnp.float32
    ).astype(jnp.bfloat16)
    receiver_columns = lax.dynamic_slice_in_dim(segment, receiver_start, block_width, 2)
    receptor_table = jnp.einsum(
        "sgb,br->srg", receiver_columns, receiver_factor, preferred_element_type=jnp.float32
    ).astype(jnp.bfloat16)
    joined_tables = jnp.concatenate([ligand_table, receptor_table], axis=1)
    ligand_rows = jnp.take(joined_tables[:, :factor_rank, :], ligand_gene, axis=2).astype(
        jnp.float32
    )
    receptor_rows = jnp.take(joined_tables[:, factor_rank:, :], receptor_gene, axis=2).astype(
        jnp.float32
    )
    pair_weights = pair_factor.astype(jnp.float32).T
    partial_product = jnp.sum(ligand_rows * receptor_rows * pair_weights[None, :, :], axis=2)
    pair_gram = jnp.einsum(
        "pr,pq->rq", pair_factor, pair_factor, preferred_element_type=jnp.float32
    )
    sender_gram = jnp.einsum(
        "pr,pq->rq", sender_factor, sender_factor, preferred_element_type=jnp.float32
    )
    receiver_gram = jnp.einsum(
        "pr,pq->rq", receiver_factor, receiver_factor, preferred_element_type=jnp.float32
    )
    product_total = lax.psum(partial_product, ("pair", "recv"))
    pair_gram = lax.psum(pair_gram, "pair")
    receiver_gram = lax.psum(receiver_gram, "recv")
    hadamard = pair_gram * sender_gram * receiver_gram
    cholesky_factor = jnp.linalg.cholesky(hadamard)
    solution = jax.scipy.linalg.cho_solve((cholesky_factor, True), product_total.T)
    return solution.T


def solution(mesh):
    placed = (
        P("samp", "recv", "pair"),
        P("samp", "recv"),
        P("pair"),
        P("pair"),
        P("pair", None),
        P(),
        P("recv", None),
    )
    return jax.shard_map(
        body, mesh=mesh, in_specs=placed, out_specs=P("samp", None), check_vma=False
    )
```

profile of v0, /device:TPU:9, one launch (start us, length us, event | category | flops | bytes accessed | tf_op | source)
XLA Modules:
  0.0 325.3 jit_solution(4889094992332328623)
XLA Ops:
  6.5 0.0 copy-start
  6.5 0.0 copy-start.2
  6.5 0.0 copy-start.3
  6.5 0.0 copy-start.1
  6.5 0.0 copy-start.4
  6.5 0.0 copy-start.5
  6.6 0.0 all-reduce.3.cloned.1.call-start
  6.6 4.6 %fusion.3 = f32[4,128,128]{1,2,0:T(8,128)} fusion(bf16[4,4096,128]{2,1,0:T(8,128)(2,1)} %param.9, s32[4,4096]{1,0:T(4,128)} %param.10), kind=kOutput, calls=%fused_computation.9 | convolution fusion | flops 538968064 | bytes 4521984 | tf_op jit(solution)/shard_map/scg,sck->sgk/dot_general | solution.py:22
  11.2 0.0 all-reduce.3.cloned.1.call-update
  11.2 0.0 all-gather.2.cloned.1.call-start
  11.3 0.0 copy-done.3
  11.3 0.2 fusion.16
  11.5 0.0 copy-done.2
  11.5 1.3 convert_reduce_fusion
  12.8 18.3 %all-reduce = (f32[4,128]{1,0:T(4,128)S(1)}, f32[32,32]{0,1:T(8,128)S(1)}) all-reduce(f32[4,128]{1,0:T(4,128)S(1)} %convert_reduce_fusion, f32[32,32]{0,1:T(8,128)S(1)} %fusion.16), channel_id=1, replica_groups=mesh['samp'=8,'pair'=16,'recv'=4] {'recv'}, use_global_device_ids=true, to_apply=%region_6.7 | all-reduce | flops 1536 | bytes 12288 | tf_op jit(solution)/shard_map/psum | solution.py:27
  31.0 43.7 %all-reduce.3.cloned.1.call-done = f32[4,128,128]{1,2,0:T(8,128)} async-done(((f32[4,128,128]{1,2,0:T(8,128)}), f32[4,128,128]{1,2,0:T(8,128)}) %all-reduce.3.cloned.1.call-update) | async-done | bytes 262160 | tf_op jit(solution)/shard_map/psum | solution.py:27
  74.7 1.7 divide_convert_fusion
  76.4 0.0 all-gather.2.cloned.1.call-update
  76.5 0.0 copy-done.1
  76.5 0.1 fusion.15
  76.6 57.9 %psum.35 = f32[32,32]{0,1:T(8,128)S(1)} all-reduce(f32[32,32]{0,1:T(8,128)S(1)} %fusion.15), channel_id=1, replica_groups=mesh['samp'=8,'pair'=16,'recv'=4] {'pair'}, use_global_device_ids=true, to_apply=%region_0.0 | all-reduce | flops 1024 | bytes 8192 | tf_op jit(solution)/shard_map/psum | solution.py:56
  134.5 0.0 copy-done
  134.5 0.1 fusion.4
  134.6 0.1 copy.16
  134.7 2.9 cholesky.16
  137.6 0.6 compare_reduce_fusion
  138.3 0.7 fusion.6
  138.9 2.5 custom-call.10
  141.4 0.1 copy.17
  141.5 0.0 copy-done.4
  141.5 0.0 copy-done.5
  141.6 0.3 all-gather.2.cloned.1.call-done
  141.8 2.0 convolution_convert_fusion
  143.8 1.4 copy.23
  145.2 1.4 convolution_convert_fusion.1
  146.6 2.5 copy.24
  149.1 0.7 gather_fusion
  149.9 2.3 gather_fusion.1
  152.2 0.3 multiply_reduce_fusion
  152.6 164.9 %psum.39 = f32[4,32]{1,0:T(4,128)S(1)} all-reduce(f32[4,32]{1,0:T(4,128)S(1)} %multiply_reduce_fusion), channel_id=1, replica_groups=mesh['samp'=8,'pair'=16,'recv'=4] {'pair','recv'}, use_global_device_ids=true, to_apply=%region_8.10 | all-reduce | flops 128 | bytes 1024 | tf_op jit(solution)/shard_map/psum | solution.py:55
  317.5 0.2 fusion.9
  317.7 0.8 fusion.7
  (9 shorter events, 0.1 us)
Async XLA Ops:
  6.5 127.9 %copy-start = (bf16[128,32]{0,1:T(8,128)(2,1)S(1)}, bf16[128,32]{0,1:T(8,128)(2,1)}, u32[]{:S(2)}) copy-start(bf16[128,32]{0,1:T(8,128)(2,1)} %param.14) | copy-start | bytes 24580
  6.5 4.9 %copy-start.2 = (s32[4,4096]{1,0:T(4,128)S(1)}, s32[4,4096]{1,0:T(4,128)}, u32[]{:S(2)}) copy-start(s32[4,4096]{1,0:T(4,128)} %param.10) | copy-start | bytes 196612
  6.5 4.7 %copy-start.3 = (bf16[32,32]{1,0:T(8,128)(2,1)S(1)}, bf16[32,32]{1,0:T(8,128)(2,1)}, u32[]{:S(2)}) copy-start(bf16[32,32]{1,0:T(8,128)(2,1)} %param.15) | copy-start | bytes 6148
  6.5 69.9 %copy-start.1 = (bf16[128,32]{0,1:T(8,128)(2,1)S(1)}, bf16[128,32]{0,1:T(8,128)(2,1)}, u32[]{:S(2)}) copy-start(bf16[128,32]{0,1:T(8,128)(2,1)} %param.13) | copy-start | bytes 24580
  6.5 134.9 %copy-start.4 = (s32[128]{0:T(128)S(1)}, s32[128]{0:T(128)}, u32[]{:S(2)}) copy-start(s32[128]{0:T(128)} %param.12) | copy-start | bytes 1540
  6.5 135.0 %copy-start.5 = (s32[128]{0:T(128)S(1)}, s32[128]{0:T(128)}, u32[]{:S(2)}) copy-start(s32[128]{0:T(128)} %param.11) | copy-start | bytes 1540
  6.6 68.1 %all-reduce.3.cloned.1.call-start = ((), (), s32[]{:S(2)}) async-start(), calls=%async_computation | async-start | bytes 524288 | tf_op jit(solution)/shard_map/psum | solution.py:27
  11.2 130.6 %all-gather.2.cloned.1.call-start = ((), (), s32[]{:S(2)}) async-start(), calls=%async_computation.1 | async-start | bytes 2228224 | tf_op jit(solution)/shard_map/all_gather | solution.py:29
Sparse Core Ops, SparseCore 0:
  11.3 63.2 all-reduce.2
  76.9 64.9 all-gather.1
where the time goes:
time: 326 us; the launch traced here: 325 us
  blocking collectives  241 us (74%)
  waiting for transfers between devices  43.9 us (13%)
  between operations  13.6 us (4%)
  other arithmetic  10.1 us (3%)
  matrix products  9.4 us (3%)
  local copies, waits for them, and re-layouts  7.17 us (2%)
    psum x1, blocking collectives, body(): product_total = lax.psum(partial_product, ('pair', 'recv'))  165 us
    psum x1, blocking collectives, body(): pair_gram = lax.psum(pair_gram, 'pair')  57.9 us
    psum x1, waiting for transfers between devices, body(): cluster_total, cell_count = lax.psum((part_sums, part_counts), 'recv')  43.7 us
    psum x1, blocking collectives, body(): cluster_total, cell_count = lax.psum((part_sums, part_counts), 'recv')  18.3 us
  transfers between devices with their start and end apart: 2, of which 2 were waited for; matrix products, arithmetic and copies ran while one was open for 3% of the time, Pallas kernels for 0%

commit v1 on v0

v1 whole, which is shorter than its diff:
```python
import jax
import jax.numpy as jnp
from jax import lax
from jax.experimental import pallas as pl
from jax.experimental.pallas import tpu as pltpu
from jax.sharding import PartitionSpec as P

F32 = jnp.float32
BF16 = jnp.bfloat16
I32 = jnp.int32
LANES = 128
STEP_CELLS = 2048
SUB_CELLS = 512


def iota(shape, dim):
    return lax.broadcasted_iota(I32, shape, dim)


def totals_kernel(clusters, x_ref, labels_ref, receiver_ref, out_ref, count_ref):
    sample, step = pl.program_id(0), pl.program_id(1)
    genes = x_ref.shape[2]

    @pl.when(step == 0)
    def _():
        out_ref[0, :clusters, :] = jnp.zeros((clusters, genes), F32)
        count_ref[...] = jnp.zeros_like(count_ref)

    cells = x_ref.shape[1]
    kinds = iota((clusters, SUB_CELLS), 0)
    total = jnp.zeros((clusters, genes), F32)
    count = jnp.zeros((clusters, LANES), F32)
    for start in range(0, cells, SUB_CELLS):
        labels = labels_ref[pl.ds(sample, 1), start : start + SUB_CELLS]
        member = jnp.where(kinds == labels, 1.0, 0.0)
        for lane in range(0, SUB_CELLS, LANES):
            count = count + member[:, lane : lane + LANES]
        total = total + jnp.dot(
            member.astype(BF16), x_ref[0, start : start + SUB_CELLS, :], preferred_element_type=F32
        )
    out_ref[0, :clusters, :] += total
    count_ref[...] += count

    @pl.when(step == pl.num_programs(1) - 1)
    def _():
        row = lax.dot_general(
            jnp.ones((8, LANES), BF16),
            count_ref[...].astype(BF16),
            (((1,), (1,)), ((), ())),
            preferred_element_type=F32,
        )
        out_ref[0, clusters : clusters + 8, :] = row
        turned = receiver_ref[...].astype(F32).T
        rank, width = turned.shape
        parts = [turned[start : start + 8, :] for start in range(0, rank, 8)]
        out_ref[0, clusters + 8 : clusters + 16, :] = jnp.concatenate(parts, axis=1)


def tables_kernel(clusters, got_ref, sender_ref, weight_ref, ligand_ref, receptor_ref, out_ref, gram_ref):
    sources, _, genes = got_ref.shape
    rank = sender_ref.shape[0]
    width = clusters // sources
    total = jnp.sum(got_ref[:, :clusters, :], axis=0)
    row = jnp.sum(got_ref[:, clusters : clusters + 1, :], axis=0)
    count = jnp.broadcast_to(jnp.maximum(row, 1.0), (clusters, clusters)).T
    mean = (total / count).astype(BF16)
    blocks = []
    for source in range(sources):
        packed = got_ref[source, clusters + 8 : clusters + 16, :]
        parts = [packed[:, start : start + width] for start in range(0, LANES, width)]
        blocks.append(jnp.concatenate(parts, axis=0))
    receiver = jnp.concatenate(blocks, axis=1).astype(BF16)
    sender = sender_ref[...]
    tables = jnp.dot(jnp.concatenate([sender, receiver], axis=0), mean, preferred_element_type=F32)
    flat = (((1,), (1,)), ((), ()))
    sender_gram = lax.dot_general(sender, sender, flat, preferred_element_type=F32)
    receiver_gram = lax.dot_general(receiver, receiver, flat, preferred_element_type=F32)
    gram_ref[...] = sender_gram * receiver_gram
    ligand, receptor = ligand_ref[...], receptor_ref[...]
    rows = [ligand >> 7, ligand & 127, receptor >> 7, receptor & 127]
    where = jnp.zeros((16, LANES), F32)
    place = iota((16, LANES), 0)
    for spot, part in enumerate(rows):
        where = jnp.where(place == spot, part.astype(F32), where)
    block = jnp.concatenate([tables.astype(BF16), weight_ref[...], where.astype(BF16)], axis=0)
    for target in range(out_ref.shape[0]):
        out_ref[target] = block


def product_kernel(rank, got_ref, gram_ref, out_ref):
    sources = got_ref.shape[0]
    halves = sources // 2
    ligand_table = jnp.concatenate(
        [
            jnp.concatenate([got_ref[2 * h, :rank, :], got_ref[2 * h + 1, :rank, :]], axis=1)
            for h in range(halves)
        ],
        axis=0,
    )
    receptor_table = jnp.concatenate(
        [
            jnp.concatenate(
                [got_ref[2 * h, rank : 2 * rank, :], got_ref[2 * h + 1, rank : 2 * rank, :]], axis=1
            )
            for h in range(halves)
        ],
        axis=0,
    )
    spots = iota((2 * LANES, 2 * LANES), 0)

    def rows_of(table, high, low):
        upper = high >> 1
        lower = low + (high & 1) * LANES
        chosen = jnp.where(spots == lower, 1.0, 0.0).astype(BF16)
        spread = jnp.dot(table, chosen, preferred_element_type=F32)
        picked = jnp.zeros((rank, 2 * LANES), F32)
        for h in range(halves):
            picked = picked + jnp.where(upper == h, spread[h * rank : (h + 1) * rank, :], 0.0)
        return picked

    product = jnp.zeros((rank, 2 * LANES), F32)
    gram = jnp.zeros((rank, rank), F32)
    for h in range(halves):
        weight = jnp.concatenate(
            [got_ref[2 * h, 2 * rank : 3 * rank, :], got_ref[2 * h + 1, 2 * rank : 3 * rank, :]], axis=1
        )
        where = jnp.concatenate(
            [got_ref[2 * h, 3 * rank : 3 * rank + 16, :], got_ref[2 * h + 1, 3 * rank : 3 * rank + 16, :]],
            axis=1,
        ).astype(F32).astype(I32)
        ligand = rows_of(ligand_table, where[0:1, :], where[1:2, :])
        receptor = rows_of(receptor_table, where[2:3, :], where[3:4, :])
        product = product + ligand * receptor * weight.astype(F32)
        gram = gram + lax.dot_general(
            weight, weight, (((1,), (1,)), ((), ())), preferred_element_type=F32
        )
    right = jnp.sum(product, axis=1, keepdims=True)
    hadamard = gram * gram_ref[...]
    work = jnp.concatenate([hadamard, jnp.broadcast_to(right, (rank, LANES - rank))], axis=1)
    rows = iota((rank, LANES), 0)
    for j in range(rank):
        pivot = work[j : j + 1, j : j + 1]
        pivot = jnp.where(pivot > 0.0, pivot, jnp.nan)
        line = work[j : j + 1, :] / pivot
        work = jnp.where(rows == j, line, work - work[:, j : j + 1] * line)
    lanes = iota((rank, LANES), 1)
    answer = jnp.sum(jnp.where(rows == lanes, work[:, rank : rank + 1], 0.0), axis=0, keepdims=True)
    out_ref[...] = jnp.broadcast_to(answer[:, :rank], out_ref.shape)


def body(
    cell_expression,
    cell_labels,
    ligand_gene,
    receptor_gene,
    pair_factor,
    sender_factor,
    receiver_factor,
):
    samples, cells, genes = cell_expression.shape
    clusters, rank = sender_factor.shape
    targets = lax.axis_size("pair")
    height = clusters + 16
    step_cells = min(STEP_CELLS, cells)
    sent = pl.pallas_call(
        lambda *refs: totals_kernel(clusters, *refs),
        grid=(samples, cells // step_cells),
        in_specs=[
            pl.BlockSpec((1, step_cells, genes), lambda s, c: (s, c, 0)),
            pl.BlockSpec((samples, step_cells), lambda s, c: (0, c)),
            pl.BlockSpec(receiver_factor.shape, lambda s, c: (0, 0)),
        ],
        out_specs=pl.BlockSpec((1, height, genes), lambda s, c: (s, 0, 0)),
        out_shape=jax.ShapeDtypeStruct((samples, height, genes), F32),
        scratch_shapes=[pltpu.VMEM((clusters, LANES), F32)],
        name="totals",
    )(cell_expression, cell_labels, receiver_factor)
    got = lax.all_to_all(sent, "recv", 0, 0, tiled=True)
    sent, gram = pl.pallas_call(
        lambda *refs: tables_kernel(clusters, *refs),
        out_shape=(
            jax.ShapeDtypeStruct((targets, 3 * rank + 16, genes), BF16),
            jax.ShapeDtypeStruct((rank, rank), F32),
        ),
        name="tables",
    )(got, sender_factor.T, pair_factor.T, ligand_gene[None, :], receptor_gene[None, :])
    got = lax.all_to_all(sent, "pair", 0, 0, tiled=True)
    sent = pl.pallas_call(
        lambda *refs: product_kernel(rank, *refs),
        out_shape=jax.ShapeDtypeStruct((samples, rank), F32),
        name="product",
    )(got, gram)
    return lax.all_to_all(sent, "recv", 0, 0, tiled=True)


def solution(mesh):
    placed = (
        P("samp", "recv", "pair"),
        P("samp", "recv"),
        P("pair"),
        P("pair"),
        P("pair", None),
        P(),
        P("recv", None),
    )
    return jax.shard_map(
        body, mesh=mesh, in_specs=placed, out_specs=P("samp", None), check_vma=False
    )
```

time: 326 us -> 68 us (0.21)
  the two profiles are of different devices: /device:TPU:9 before, /device:TPU:1 now
where the time goes in v1:
time: 68 us; the launch traced here: 67.5 us
  blocking collectives  51.8 us (76%)
  Pallas kernels  15.1 us (22%)
    all_to_all x1, blocking collectives, body(): got = lax.all_to_all(sent, 'recv', 0, 0, tiled=True)  20.8 us
    all_to_all x1, blocking collectives, body(): got = lax.all_to_all(sent, 'pair', 0, 0, tiled=True)  18 us
    all_to_all x1, blocking collectives, body(): return lax.all_to_all(sent, 'recv', 0, 0, tiled=True)  13 us
    pallas_call x1, Pallas kernels, body(): pl.pallas_call(lambda *refs: totals_kernel(clusters, *refs), grid=(sample...  7.49 us
    pallas_call x1, Pallas kernels, body(): pl.pallas_call(lambda *refs: product_kernel(rank, *refs), out_shape=jax.S...  5.53 us
    pallas_call x1, Pallas kernels, body(): pl.pallas_call(lambda *refs: tables_kernel(clusters, *refs), out_shape=(j...  2.04 us

profile of v1, /device:TPU:1, one launch (start us, length us, event | category | flops | bytes accessed | tf_op | source)
XLA Modules:
  0.0 67.5 jit_solution(7729631948236040309)
XLA Ops:
  0.0 7.5 %totals.1 = f32[4,144,128]{2,1,0:T(8,128)} custom-call(bf16[4,4096,128]{2,1,0:T(8,128)(2,1)} %refs_0_.1, s32[4,4096]{1,0:T(4,128)} %refs_1_.1, bf16[32,32]{1,0:T(8,128)(2,1)} %refs_2_.1), custom_call_target="tpu_custom_call" | custom-call | tf_op jit(solution)/shard_map/totals/pallas_call | solution.py:165
  7.5 20.8 %all_to_all.22.refs_0_ = f32[4,144,128]{2,1,0:T(8,128)} all-to-all(f32[4,144,128]{2,1,0:T(8,128)} %totals.1), channel_id=1, replica_groups=mesh['samp'=8,'pair'=16,'recv'=4] {'recv'}, dimensions={0} | all-to-all | bytes 589824 | tf_op jit(solution)/shard_map/all_to_all | solution.py:178
  28.2 2.0 %tables.1 = (bf16[16,112,128]{2,1,0:T(8,128)(2,1)}, f32[32,32]{1,0:T(8,128)}) custom-call(f32[4,144,128]{2,1,0:T(8,128)} %all_to_all.22.refs_0_, bf16[32,128]{1,0:T(8,128)(2,1)} %bitcast.9, bf16[32,128]{1,0:T(8,128)(2,1)} %bitcast.10, s32[1,128]{1,0:T(1,128)} %bitcast.12, s32[1,128]{1,0:T(1,128)} %bitcast.13), custom_call_target="tpu_custom_call" | custom-call | tf_op jit(solution)/shard_map/tables/pallas_call | solution.py:179
  30.3 18.0 %all_to_all.23.refs_0_ = bf16[16,112,128]{2,1,0:T(8,128)(2,1)} all-to-all(bf16[16,112,128]{2,1,0:T(8,128)(2,1)} %get-tuple-element.7), channel_id=1, replica_groups=mesh['samp'=8,'pair'=16,'recv'=4] {'pair'}, dimensions={0} | all-to-all | bytes 917504 | tf_op jit(solution)/shard_map/all_to_all | solution.py:187
  48.3 5.5 %product.1 = f32[4,32]{1,0:T(4,128)} custom-call(bf16[16,112,128]{2,1,0:T(8,128)(2,1)} %all_to_all.23.refs_0_, f32[32,32]{1,0:T(8,128)} %get-tuple-element.8.refs_1_), custom_call_target="tpu_custom_call" | custom-call | tf_op jit(solution)/shard_map/product/pallas_call | solution.py:188
  53.9 13.0 %all_to_all.24 = f32[4,1,32]{2,1,0:T(1,128)S(1)} all-to-all(f32[4,1,32]{2,1,0:T(1,128)} %bitcast.8), channel_id=1, replica_groups=mesh['samp'=8,'pair'=16,'recv'=4] {'recv'}, dimensions={0} | all-to-all | bytes 1024 | tf_op jit(solution)/shard_map/all_to_all | solution.py:193
  66.9 0.6 copy.10

commit v2 on v0

v2 whole, which is shorter than its diff:
```python
import jax
import jax.numpy as jnp
from jax import lax
from jax.experimental import pallas as pl
from jax.experimental.pallas import tpu as pltpu
from jax.sharding import Mesh
from jax.sharding import PartitionSpec as P

F32 = jnp.float32
BF16 = jnp.bfloat16
I32 = jnp.int32
LANES = 128
CHUNK = 512
ROW_PAIRS = (((1,), (1,)), ((), ()))


def iota(shape, dim):
    return lax.broadcasted_iota(I32, shape, dim)


def totals_kernel(
    x_hbm, labels_hbm, receiver_hbm, sender_hbm, weight_hbm, ligand_hbm, receptor_hbm,
    sums_ref, side_ref, sender_ref,
    x_ref, labels_ref, receiver_ref, weight_ref, ligand_ref, receptor_ref, x_sem, sems,
):
    samples, cells, genes = x_ref.shape
    rank, clusters = sender_ref.shape
    small = [
        pltpu.make_async_copy(source, target, sems.at[spot])
        for spot, (source, target) in enumerate(
            [
                (labels_hbm, labels_ref),
                (receiver_hbm, receiver_ref),
                (sender_hbm, sender_ref),
                (weight_hbm, weight_ref),
                (ligand_hbm, ligand_ref),
                (receptor_hbm, receptor_ref),
            ]
        )
    ]
    small[0].start()
    halves = [(0, samples // 2), (samples // 2, samples)]
    large = [
        pltpu.make_async_copy(x_hbm.at[pl.ds(a, b - a)], x_ref.at[pl.ds(a, b - a)], x_sem.at[i])
        for i, (a, b) in enumerate(halves)
    ]
    for copy in large:
        copy.start()
    for copy in small[1:]:
        copy.start()
    for copy in small:
        copy.wait()
    turned = receiver_ref[...].astype(F32).T
    parts = [turned[start : start + 8, :] for start in range(0, rank, 8)]
    packed = jnp.concatenate(parts, axis=1)
    side_ref[:rank, :] = weight_ref[...]
    ligand, receptor = ligand_ref[...], receptor_ref[...]
    digits = [ligand >> 7, ligand & 127, receptor >> 7, receptor & 127]
    place = iota((8, LANES), 0)
    where = jnp.zeros((8, LANES), F32)
    for spot, digit in enumerate(digits):
        where = jnp.where(place == spot, digit.astype(F32), where)
    side_ref[rank:, :] = where.astype(BF16)
    kinds = iota((clusters, CHUNK), 0).astype(F32).astype(BF16)
    one, zero = jnp.ones((), BF16), jnp.zeros((), BF16)
    for (first, last), copy in zip(halves, large):
        members = {}
        for sample in range(first, last):
            count = jnp.zeros((clusters, LANES), BF16)
            for start in range(0, cells, CHUNK):
                labels = labels_ref[sample : sample + 1, start : start + CHUNK].astype(F32)
                labels = jnp.broadcast_to(labels, (16, CHUNK)).astype(BF16)
                labels = jnp.concatenate([labels] * (clusters // 16), axis=0)
                member = jnp.where(kinds == labels, one, zero)
                for lane in range(0, CHUNK, LANES):
                    count = count + member[:, lane : lane + LANES]
                members[sample, start] = member
            row = lax.dot_general(
                jnp.ones((8, LANES), BF16), count, ROW_PAIRS, preferred_element_type=F32
            )
            sums_ref[sample, clusters : clusters + 8, :] = row
            sums_ref[sample, clusters + 8 :, :] = packed
        copy.wait()
        for sample in range(first, last):
            total = jnp.zeros((clusters, genes), F32)
            for start in range(0, cells, CHUNK):
                total = total + jnp.dot(
                    members[sample, start],
                    x_ref[sample, start : start + CHUNK, :],
                    preferred_element_type=F32,
                )
            sums_ref[sample, :clusters, :] = total


def tables_kernel(got_ref, sender_ref, side_ref, out_ref, gram_ref):
    sources = got_ref.shape[0]
    rank, clusters = sender_ref.shape
    targets, parts = out_ref.shape[0], rank // 8
    width = clusters // sources
    total = jnp.sum(got_ref[:, :clusters, :], axis=0)
    row = jnp.sum(got_ref[:, clusters : clusters + 1, :], axis=0)
    count = jnp.broadcast_to(jnp.maximum(row, 1.0), (clusters, clusters)).T
    mean = (total / count).astype(BF16)
    blocks = []
    for source in range(sources):
        packed = got_ref[source, clusters + 8 : clusters + 16, :]
        pieces = [packed[:, start : start + width] for start in range(0, LANES, width)]
        blocks.append(jnp.concatenate(pieces, axis=0))
    receiver = jnp.concatenate(blocks, axis=1).astype(BF16)
    sender = sender_ref[...]
    tables = jnp.dot(jnp.concatenate([sender, receiver], axis=0), mean, preferred_element_type=F32)
    side = side_ref[...]
    for part in range(parts):
        low = part * 8
        both = [tables[low : low + 8, :], tables[rank + low : rank + low + 8, :]]
        both = jnp.concatenate(both, axis=0).astype(BF16)
        for target in range(part * (targets // parts), (part + 1) * (targets // parts)):
            out_ref[target, :16, :] = both
            out_ref[target, 16:, :] = side
    sender_gram = lax.dot_general(sender, sender, ROW_PAIRS, preferred_element_type=F32)
    receiver_gram = lax.dot_general(receiver, receiver, ROW_PAIRS, preferred_element_type=F32)
    gram_ref[...] = sender_gram * receiver_gram


def product_kernel(rank, got_ref, out_ref):
    sources = got_ref.shape[0]
    part = lax.axis_index("part")
    tables = [got_ref[source, :16, :].astype(F32) for source in range(sources)]
    product = jnp.zeros((8, LANES), F32)
    for source in range(sources):
        weights = got_ref[source, 16 : 16 + rank, :].astype(F32)
        weight = weights[:8, :]
        for other in range(1, rank // 8):
            weight = jnp.where(part == other, weights[other * 8 : other * 8 + 8, :], weight)
        where = got_ref[source, 16 + rank : 24 + rank, :].astype(F32).astype(I32)
        digits = [jnp.broadcast_to(where[spot : spot + 1, :], (8, LANES)) for spot in range(4)]
        ligand = jnp.zeros((8, LANES), F32)
        receptor = jnp.zeros((8, LANES), F32)
        for block in range(sources):
            found = jnp.take_along_axis(tables[block][:8, :], digits[1], axis=1)
            ligand = jnp.where(digits[0] == block, found, ligand)
            found = jnp.take_along_axis(tables[block][8:, :], digits[3], axis=1)
            receptor = jnp.where(digits[2] == block, found, receptor)
        product = product + ligand * receptor * weight
    column = jnp.sum(product, axis=1, keepdims=True)
    line = jnp.where(iota((8, LANES), 0) == iota((8, LANES), 1), column, 0.0)
    line = jnp.sum(line, axis=0, keepdims=True)
    for target in range(out_ref.shape[0]):
        out_ref[target] = line


def inverse_kernel(got_ref, gram_ref, out_ref):
    rank = gram_ref.shape[0]
    gram = jnp.zeros((rank, rank), F32)
    for source in range(got_ref.shape[0]):
        weight = got_ref[source, 16 : 16 + rank, :]
        gram = gram + lax.dot_general(weight, weight, ROW_PAIRS, preferred_element_type=F32)
    hadamard = gram * gram_ref[...]
    rows, lanes = iota((rank, LANES), 0), iota((rank, LANES), 1)
    unit = jnp.where(iota((rank, LANES - rank), 0) == iota((rank, LANES - rank), 1), 1.0, 0.0)
    work = jnp.concatenate([hadamard, unit], axis=1)
    for j in range(rank):
        pivot = work[j : j + 1, j : j + 1]
        pivot = jnp.where(pivot > 0.0, pivot, jnp.nan)
        line = work[j : j + 1, :] / pivot
        work = jnp.where(rows == j, line, work - work[:, j : j + 1] * line)
    out_ref[...] = work[:, rank : 2 * rank]


def apply_kernel(samples, got_ref, inverse_ref, out_ref):
    rank = inverse_ref.shape[0]
    parts = got_ref.shape[0] // samples
    lines = []
    for sample in range(samples):
        pieces = [got_ref[part * samples + sample, :, :8] for part in range(parts)]
        lines.append(jnp.concatenate(pieces, axis=1))
    product = jnp.concatenate(lines + [jnp.zeros((8 - samples, rank), F32)], axis=0)
    answer = jnp.dot(
        product, inverse_ref[...], precision=lax.Precision.HIGHEST, preferred_element_type=F32
    )
    out_ref[...] = answer[:samples, :]


def on_chip(array):
    return pltpu.with_memory_space_constraint(array, pltpu.VMEM)


def body(
    cell_expression,
    cell_labels,
    ligand_gene,
    receptor_gene,
    pair_factor,
    sender_factor,
    receiver_factor,
):
    samples, cells, genes = cell_expression.shape
    clusters, rank = sender_factor.shape
    parts = lax.axis_size("part")
    targets = parts * lax.axis_size("line")
    anywhere = pl.BlockSpec(memory_space=pl.ANY)
    vmem = pl.BlockSpec(memory_space=pltpu.VMEM)
    sums, side, sender = pl.pallas_call(
        totals_kernel,
        in_specs=[anywhere] * 7,
        out_specs=(vmem, vmem, vmem),
        out_shape=(
            pltpu.VMEM((samples, clusters + 16, genes), F32),
            pltpu.VMEM((rank + 8, LANES), BF16),
            pltpu.VMEM((rank, clusters), BF16),
        ),
        scratch_shapes=[
            pltpu.VMEM((samples, cells, genes), BF16),
            pltpu.VMEM((samples, cells), I32),
            pltpu.VMEM(receiver_factor.shape, BF16),
            pltpu.VMEM((rank, LANES), BF16),
            pltpu.VMEM((1, LANES), I32),
            pltpu.VMEM((1, LANES), I32),
            pltpu.SemaphoreType.DMA((2,)),
            pltpu.SemaphoreType.DMA((6,)),
        ],
        name="totals",
    )(
        cell_expression,
        cell_labels,
        receiver_factor,
        sender_factor.T,
        pair_factor.T,
        ligand_gene[None, :],
        receptor_gene[None, :],
    )
    side, sender = on_chip(side), on_chip(sender)
    got = on_chip(lax.all_to_all(sums, "recv", 0, 0, tiled=True))
    sent, gram = pl.pallas_call(
        tables_kernel,
        in_specs=[vmem] * 3,
        out_specs=(vmem, vmem),
        out_shape=(
            pltpu.VMEM((targets, rank + 24, genes), BF16),
            pltpu.VMEM((rank, rank), F32),
        ),
        name="tables",
    )(got, sender, side)
    got = on_chip(lax.all_to_all(sent, ("part", "line"), 0, 0, tiled=True))
    sent = pl.pallas_call(
        lambda *refs: product_kernel(rank, *refs),
        in_specs=[vmem],
        out_specs=vmem,
        out_shape=pltpu.VMEM((parts * samples, 1, LANES), F32),
        name="product",
    )(got)
    final = on_chip(lax.all_to_all(sent, ("part", "recv"), 0, 0, tiled=True))
    inverse = pl.pallas_call(
        inverse_kernel,
        in_specs=[vmem] * 2,
        out_specs=vmem,
        out_shape=pltpu.VMEM((rank, rank), F32),
        name="inverse",
    )(got, on_chip(gram))
    return pl.pallas_call(
        lambda *refs: apply_kernel(samples, *refs),
        in_specs=[vmem] * 2,
        out_specs=vmem,
        out_shape=jax.ShapeDtypeStruct((samples, rank), F32),
        name="apply",
    )(final, on_chip(inverse))


def solution(mesh):
    samp, pair, recv = mesh.devices.shape
    split = Mesh(mesh.devices.reshape(samp, 4, pair // 4, recv), ("samp", "part", "line", "recv"))
    pairs = ("part", "line")
    placed = (
        P("samp", "recv", pairs),
        P("samp", "recv"),
        P(pairs),
        P(pairs),
        P(pairs, None),
        P(),
        P("recv", None),
    )
    return jax.shard_map(
        body, mesh=split, in_specs=placed, out_specs=P("samp", None), check_vma=False
    )
```

time: 326 us -> 53.4 us (0.16)
  the two profiles are of different devices: /device:TPU:9 before, /device:TPU:1 now
where the time goes in v2:
time: 53.4 us; the launch traced here: 53.2 us
  blocking collectives  34.5 us (65%)
  Pallas kernels  9.37 us (18%)
  starting transfers between devices  5.27 us (10%)
  waiting for transfers between devices  4.01 us (8%)
    all_to_all x1, blocking collectives, body(): got = on_chip(lax.all_to_all(sums, 'recv', 0, 0, tiled=True))  19.6 us
    all_to_all x1, blocking collectives, body(): got = on_chip(lax.all_to_all(sent, ('part', 'line'), 0, 0, tiled=True))  14.9 us
    all_to_all x1, starting transfers between devices, body(): final = on_chip(lax.all_to_all(sent, ('part', 'recv'), 0, 0, tiled=True))  5.27 us
    pallas_call x1, Pallas kernels, body(): pl.pallas_call(totals_kernel, in_specs=[anywhere] * 7, out_specs=(vmem, v...  4.02 us
    all_to_all x1, waiting for transfers between devices, body(): final = on_chip(lax.all_to_all(sent, ('part', 'recv'), 0, 0, tiled=True))  4.01 us
    pallas_call x1, Pallas kernels, body(): pl.pallas_call(inverse_kernel, in_specs=[vmem] * 2, out_specs=vmem, out_s...  2.98 us
    pallas_call x1, Pallas kernels, body(): pl.pallas_call(lambda *refs: product_kernel(rank, *refs), in_specs=[vmem]...  1.31 us
  transfers between devices with their start and end apart: 1, of which 1 were waited for; matrix products, arithmetic and copies ran while one was open for 0% of the time, Pallas kernels for 6%

profile of v2, /device:TPU:1, one launch (start us, length us, event | category | flops | bytes accessed | tf_op | source)
XLA Modules:
  0.0 53.2 jit_solution(5848250597659410888)
XLA Ops:
  0.0 4.0 %totals.1 = (f32[4,144,128]{2,1,0:T(8,128)S(1)}, bf16[40,128]{1,0:T(8,128)(2,1)S(1)}, bf16[32,128]{1,0:T(8,128)(2,1)S(1)}) custom-call(bf16[4,4096,128]{2,1,0:T(8,128)(2,1)} %x_hbm.1, s32[4,4096]{1,0:T(4,128)} %labels_hbm.1, bf16[32,32]{1,0:T(8,128)(2,1)} %receiver_hbm.1, bf16[32,128]{1,0:T(8,128)(2,1)} %bitcast.4, bf16[32,128]{1,0:T(8,128)(2,1)} %bitcast.5, ...), custom_call_target="tpu_custom_call" | custom-call | tf_op jit(solution)/shard_map/totals/pallas_call | solution.py:203
  4.0 19.6 %all_to_all.15.got_ref = f32[4,144,128]{2,1,0:T(8,128)S(1)} all-to-all(f32[4,144,128]{2,1,0:T(8,128)S(1)} %get-tuple-element.10), channel_id=1, replica_groups=mesh['samp'=8,'part'=4,'line'=4,'recv'=4] {'recv'}, dimensions={0} | all-to-all | bytes 589824 | tf_op jit(solution)/shard_map/all_to_all | solution.py:233
  23.6 0.3 tables.1
  23.9 14.9 %all_to_all.16.refs_0_.got_ref = bf16[16,56,128]{2,1,0:T(8,128)(2,1)S(1)} all-to-all(bf16[16,56,128]{2,1,0:T(8,128)(2,1)S(1)} %get-tuple-element.13), channel_id=1, replica_groups=mesh['samp'=8,'part'=4,'line'=4,'recv'=4] {'part','line'}, dimensions={0} | all-to-all | bytes 458752 | tf_op jit(solution)/shard_map/all_to_all | solution.py:244
  38.8 1.3 %product.1 = f32[16,1,128]{2,1,0:T(1,128)} custom-call(bf16[16,56,128]{2,1,0:T(8,128)(2,1)S(1)} %all_to_all.16.refs_0_.got_ref), custom_call_target="tpu_custom_call" | custom-call | tf_op jit(solution)/shard_map/product/pallas_call | solution.py:245
  40.1 5.3 %all-to-all-start.2 = ((f32[16,1,128]{2,1,0:T(1,128)}), f32[16,1,128]{2,1,0:T(1,128)S(1)}, u32[]{:S(2)}, u32[]{:S(2)}) async-start(f32[16,1,128]{2,1,0:T(1,128)} %product.1), calls=%async_computation.2 | async-start | bytes 16384 | tf_op jit(solution)/shard_map/all_to_all | solution.py:252
  45.4 3.0 %inverse.1.refs_1_ = f32[32,32]{1,0:T(8,128)S(1)} custom-call(bf16[16,56,128]{2,1,0:T(8,128)(2,1)S(1)} %all_to_all.16.refs_0_.got_ref, f32[32,32]{1,0:T(8,128)S(1)} %get-tuple-element.14.gram_ref), custom_call_target="tpu_custom_call" | custom-call | tf_op jit(solution)/shard_map/inverse/pallas_call | solution.py:253
  48.4 4.0 %all-to-all-done.2.refs_0_ = f32[16,1,128]{2,1,0:T(1,128)S(1)} async-done(((f32[16,1,128]{2,1,0:T(1,128)}), f32[16,1,128]{2,1,0:T(1,128)S(1)}, u32[]{:S(2)}, u32[]{:S(2)}) %all-to-all-start.2) | async-done | bytes 8224 | tf_op jit(solution)/shard_map/all_to_all | solution.py:252
  52.4 0.8 %apply.1 = f32[4,32]{1,0:T(4,128)} custom-call(f32[16,1,128]{2,1,0:T(1,128)S(1)} %all-to-all-done.2.refs_0_, f32[32,32]{1,0:T(8,128)S(1)} %inverse.1.refs_1_), custom_call_target="tpu_custom_call" | custom-call | tf_op jit(solution)/shard_map/apply/pallas_call | solution.py:260
Async XLA Ops:
  40.1 12.3 %all-to-all-start.2 = ((f32[16,1,128]{2,1,0:T(1,128)}), f32[16,1,128]{2,1,0:T(1,128)S(1)}, u32[]{:S(2)}, u32[]{:S(2)}) async-start(f32[16,1,128]{2,1,0:T(1,128)} %product.1), calls=%async_computation.2 | async-start | bytes 16384 | tf_op jit(solution)/shard_map/all_to_all | solution.py:252

commit v3 on v2

--- a/solution.py
+++ b/solution.py
@@ -48,23 +48,12 @@
         copy.start()
     for copy in small[1:]:
         copy.start()
-    for copy in small:
-        copy.wait()
-    turned = receiver_ref[...].astype(F32).T
-    parts = [turned[start : start + 8, :] for start in range(0, rank, 8)]
-    packed = jnp.concatenate(parts, axis=1)
-    side_ref[:rank, :] = weight_ref[...]
-    ligand, receptor = ligand_ref[...], receptor_ref[...]
-    digits = [ligand >> 7, ligand & 127, receptor >> 7, receptor & 127]
-    place = iota((8, LANES), 0)
-    where = jnp.zeros((8, LANES), F32)
-    for spot, digit in enumerate(digits):
-        where = jnp.where(place == spot, digit.astype(F32), where)
-    side_ref[rank:, :] = where.astype(BF16)
+    small[0].wait()
     kinds = iota((clusters, CHUNK), 0).astype(F32).astype(BF16)
     one, zero = jnp.ones((), BF16), jnp.zeros((), BF16)
+    extras = {}
     for (first, last), copy in zip(halves, large):
-        members = {}
+        members, counts = {}, {}
         for sample in range(first, last):
             count = jnp.zeros((clusters, LANES), BF16)
             for start in range(0, cells, CHUNK):
@@ -77,9 +66,16 @@
                 members[sample, start] = member
             row = lax.dot_general(
                 jnp.ones((8, LANES), BF16), count, ROW_PAIRS, preferred_element_type=F32
+            ).astype(I32)
+            row = jnp.where(iota((8, LANES), 0) == 0, row - (row & 255), row & 255)
+            extras[sample] = row.astype(F32)
+            counts[sample] = jnp.dot(
+                count, jnp.ones((LANES, genes), BF16), preferred_element_type=F32
             )
-            sums_ref[sample, clusters : clusters + 8, :] = row
-            sums_ref[sample, clusters + 8 :, :] = packed
+        if first:
+            for other in small[1:]:
+                other.wait()
+            fill_side(weight_ref, ligand_ref, receptor_ref, side_ref)
         copy.wait()
         for sample in range(first, last):
             total = jnp.zeros((clusters, genes), F32)
@@ -89,7 +85,38 @@
                     x_ref[sample, start : start + CHUNK, :],
                     preferred_element_type=F32,
                 )
-            sums_ref[sample, :clusters, :] = total
+            level = jnp.sum(total, axis=0, keepdims=True) * (1.0 / cells)
+            level = level.astype(BF16).astype(F32)
+            sums_ref[sample, :clusters, :] = (total - counts[sample] * level).astype(BF16)
+            extras[sample] = jnp.where(iota((8, LANES), 0) == 2, level, extras[sample])
+    turned = receiver_ref[...].astype(F32).T
+    packed = jnp.concatenate([turned[start : start + 8, :] for start in range(0, rank, 8)], axis=1)
+    for sample, extra in extras.items():
+        sums_ref[sample, clusters:, :] = jnp.concatenate([extra, packed], axis=0).astype(BF16)
+
+
+def fill_side(weight_ref, ligand_ref, receptor_ref, side_ref):
+    rank = weight_ref.shape[0]
+    parts = rank // 8
+    weight = weight_ref[...]
+    gram = lax.dot_general(weight, weight, ROW_PAIRS, preferred_element_type=F32)
+    terms = []
+    for _ in range(3):
+        term = gram.astype(BF16).astype(F32)
+        gram = gram - term
+        terms += [term[8 * part : 8 * part + 8, 8 * part :] for part in range(parts)]
+    terms = jnp.concatenate(terms, axis=1)
+    terms = jnp.concatenate([terms, jnp.zeros((8, 2 * LANES - terms.shape[1]), F32)], axis=1)
+    ligand, receptor = ligand_ref[...], receptor_ref[...]
+    digits = [ligand >> 7, ligand & 127, receptor >> 7, receptor & 127]
+    place = iota((8, LANES), 0)
+    where = jnp.zeros((8, LANES), F32)
+    for spot, digit in enumerate(digits):
+        where = jnp.where(place == spot, digit.astype(F32), where)
+    weight = weight.astype(F32)
+    for part in range(parts):
+        pieces = [weight[8 * part : 8 * part + 8, :], where, terms[:, :LANES], terms[:, LANES:]]
+        side_ref[part] = jnp.concatenate(pieces, axis=0).astype(BF16)
 
 
 def tables_kernel(got_ref, sender_ref, side_ref, out_ref, gram_ref):
@@ -97,23 +124,28 @@
     rank, clusters = sender_ref.shape
     targets, parts = out_ref.shape[0], rank // 8
     width = clusters // sources
-    total = jnp.sum(got_ref[:, :clusters, :], axis=0)
-    row = jnp.sum(got_ref[:, clusters : clusters + 1, :], axis=0)
-    count = jnp.broadcast_to(jnp.maximum(row, 1.0), (clusters, clusters)).T
+    extras = [got_ref[source, clusters:, :].astype(F32) for source in range(sources)]
+    digits = jnp.concatenate([extra[:2, :] for extra in extras], axis=0).astype(BF16)
+    levels = [jnp.broadcast_to(extra[2:3, :], (2, LANES)) for extra in extras]
+    levels = jnp.concatenate(levels, axis=0).astype(BF16)
+    levels = jnp.concatenate([levels, jnp.ones_like(levels)], axis=1)
+    known = lax.dot_general(digits, levels, (((0,), (0,)), ((), ())), preferred_element_type=F32)
+    count = jnp.maximum(known[:, LANES:], 1.0)
+    total = known[:, :LANES] + jnp.sum(got_ref[:, :clusters, :].astype(F32), axis=0)
     mean = (total / count).astype(BF16)
     blocks = []
-    for source in range(sources):
-        packed = got_ref[source, clusters + 8 : clusters + 16, :]
+    for extra in extras:
+        packed = extra[8:, :]
         pieces = [packed[:, start : start + width] for start in range(0, LANES, width)]
         blocks.append(jnp.concatenate(pieces, axis=0))
     receiver = jnp.concatenate(blocks, axis=1).astype(BF16)
     sender = sender_ref[...]
     tables = jnp.dot(jnp.concatenate([sender, receiver], axis=0), mean, preferred_element_type=F32)
-    side = side_ref[...]
     for part in range(parts):
         low = part * 8
         both = [tables[low : low + 8, :], tables[rank + low : rank + low + 8, :]]
         both = jnp.concatenate(both, axis=0).astype(BF16)
+        side = side_ref[part]
         for target in range(part * (targets // parts), (part + 1) * (targets // parts)):
             out_ref[target, :16, :] = both
             out_ref[target, 16:, :] = side
@@ -122,17 +154,13 @@
     gram_ref[...] = sender_gram * receiver_gram
 
 
-def product_kernel(rank, got_ref, out_ref):
+def product_kernel(got_ref, out_ref):
     sources = got_ref.shape[0]
-    part = lax.axis_index("part")
     tables = [got_ref[source, :16, :].astype(F32) for source in range(sources)]
     product = jnp.zeros((8, LANES), F32)
     for source in range(sources):
-        weights = got_ref[source, 16 : 16 + rank, :].astype(F32)
-        weight = weights[:8, :]
-        for other in range(1, rank // 8):
-            weight = jnp.where(part == other, weights[other * 8 : other * 8 + 8, :], weight)
-        where = got_ref[source, 16 + rank : 24 + rank, :].astype(F32).astype(I32)
+        side = got_ref[source, 16:32, :].astype(F32)
+        where = side[8:, :].astype(I32)
         digits = [jnp.broadcast_to(where[spot : spot + 1, :], (8, LANES)) for spot in range(4)]
         ligand = jnp.zeros((8, LANES), F32)
         receptor = jnp.zeros((8, LANES), F32)
@@ -141,7 +169,7 @@
             ligand = jnp.where(digits[0] == block, found, ligand)
             found = jnp.take_along_axis(tables[block][8:, :], digits[3], axis=1)
             receptor = jnp.where(digits[2] == block, found, receptor)
-        product = product + ligand * receptor * weight
+        product = product + ligand * receptor * side[:8, :]
     column = jnp.sum(product, axis=1, keepdims=True)
     line = jnp.where(iota((8, LANES), 0) == iota((8, LANES), 1), column, 0.0)
     line = jnp.sum(line, axis=0, keepdims=True)
@@ -151,12 +179,23 @@
 
 def inverse_kernel(got_ref, gram_ref, out_ref):
     rank = gram_ref.shape[0]
-    gram = jnp.zeros((rank, rank), F32)
-    for source in range(got_ref.shape[0]):
-        weight = got_ref[source, 16 : 16 + rank, :]
-        gram = gram + lax.dot_general(weight, weight, ROW_PAIRS, preferred_element_type=F32)
+    parts = rank // 8
+    terms = jnp.sum(got_ref[:, 32:, :].astype(F32), axis=0)
+    terms = jnp.concatenate([terms[:8, :], terms[8:, :]], axis=1)
+    wide = sum(range(8, rank + 8, 8))
+    upper = terms[:, :wide] + terms[:, wide : 2 * wide] + terms[:, 2 * wide : 3 * wide]
+    lines, start = [], 0
+    for part in range(parts):
+        width = rank - 8 * part
+        line = upper[:, start : start + width]
+        if part:
+            line = jnp.concatenate([jnp.zeros((8, 8 * part), F32), line], axis=1)
+        lines.append(line)
+        start += width
+    upper = jnp.concatenate(lines, axis=0)
+    gram = jnp.where(iota((rank, rank), 0) <= iota((rank, rank), 1), upper, upper.T)
     hadamard = gram * gram_ref[...]
-    rows, lanes = iota((rank, LANES), 0), iota((rank, LANES), 1)
+    rows = iota((rank, LANES), 0)
     unit = jnp.where(iota((rank, LANES - rank), 0) == iota((rank, LANES - rank), 1), 1.0, 0.0)
     work = jnp.concatenate([hadamard, unit], axis=1)
     for j in range(rank):
@@ -205,8 +244,8 @@
         in_specs=[anywhere] * 7,
         out_specs=(vmem, vmem, vmem),
         out_shape=(
-            pltpu.VMEM((samples, clusters + 16, genes), F32),
-            pltpu.VMEM((rank + 8, LANES), BF16),
+            pltpu.VMEM((samples, clusters + 16, genes), BF16),
+            pltpu.VMEM((rank // 8, 32, LANES), BF16),
             pltpu.VMEM((rank, clusters), BF16),
         ),
         scratch_shapes=[
@@ -236,20 +275,20 @@
         in_specs=[vmem] * 3,
         out_specs=(vmem, vmem),
         out_shape=(
-            pltpu.VMEM((targets, rank + 24, genes), BF16),
+            pltpu.VMEM((targets, 48, genes), BF16),
             pltpu.VMEM((rank, rank), F32),
         ),
         name="tables",
     )(got, sender, side)
     got = on_chip(lax.all_to_all(sent, ("part", "line"), 0, 0, tiled=True))
     sent = pl.pallas_call(
-        lambda *refs: product_kernel(rank, *refs),
+        product_kernel,
         in_specs=[vmem],
         out_specs=vmem,
         out_shape=pltpu.VMEM((parts * samples, 1, LANES), F32),
         name="product",
     )(got)
-    final = on_chip(lax.all_to_all(sent, ("part", "recv"), 0, 0, tiled=True))
+    final = on_chip(lax.all_to_all(on_chip(sent), ("part", "recv"), 0, 0, tiled=True))
     inverse = pl.pallas_call(
         inverse_kernel,
         in_specs=[vmem] * 2,

time: 53.4 us -> 49.3 us (0.923)
  blocking collectives: 34.5 us -> 30.9 us
    all_to_all x1, blocking collectives: 19.6 us -> 17.5 us  [body(): got = on_chip(lax.all_to_all(sums, 'recv', 0, 0, tiled=True))]
    all_to_all x1, blocking collectives: 14.9 us -> 13.5 us  [body(): got = on_chip(lax.all_to_all(sent, ('part', 'line'), 0, 0, tiled=True))]
where the time goes in v3:
time: 49.3 us; the launch traced here: 49.1 us
  blocking collectives  30.9 us (63%)
  Pallas kernels  9.03 us (18%)
  starting transfers between devices  5.14 us (10%)
  waiting for transfers between devices  3.98 us (8%)
    all_to_all x1, blocking collectives, body(): got = on_chip(lax.all_to_all(sums, 'recv', 0, 0, tiled=True))  17.5 us
    all_to_all x1, blocking collectives, body(): got = on_chip(lax.all_to_all(sent, ('part', 'line'), 0, 0, tiled=True))  13.5 us
    all_to_all x1, starting transfers between devices, body(): lax.all_to_all(on_chip(sent), ('part', 'recv'), 0, 0, tiled=True)  5.14 us
    all_to_all x1, waiting for transfers between devices, body(): lax.all_to_all(on_chip(sent), ('part', 'recv'), 0, 0, tiled=True)  3.98 us
    pallas_call x1, Pallas kernels, body(): pl.pallas_call(totals_kernel, in_specs=[anywhere] * 7, out_specs=(vmem, v...  3.57 us
    pallas_call x1, Pallas kernels, body(): pl.pallas_call(inverse_kernel, in_specs=[vmem] * 2, out_specs=vmem, out_s...  3.02 us
    pallas_call x1, Pallas kernels, body(): pl.pallas_call(product_kernel, in_specs=[vmem], out_specs=vmem, out_shape...  1.31 us
  transfers between devices with their start and end apart: 1, of which 1 were waited for; matrix products, arithmetic and copies ran while one was open for 0% of the time, Pallas kernels for 6%

profile of v3, /device:TPU:1, one launch (start us, length us, event | category | flops | bytes accessed | tf_op | source)
XLA Modules:
  0.0 49.1 jit_solution(11278021030771283375)
XLA Ops:
  0.0 3.6 %totals.1 = (bf16[4,144,128]{2,1,0:T(8,128)(2,1)S(1)}, bf16[4,32,128]{2,1,0:T(8,128)(2,1)S(1)}, bf16[32,128]{1,0:T(8,128)(2,1)S(1)}) custom-call(bf16[4,4096,128]{2,1,0:T(8,128)(2,1)} %x_hbm.1, s32[4,4096]{1,0:T(4,128)} %labels_hbm.1, bf16[32,32]{1,0:T(8,128)(2,1)} %receiver_hbm.1, bf16[32,128]{1,0:T(8,128)(2,1)} %bitcast.4, bf16[32,128]{1,0:T(8,128)(2,1)} %bitcast.5, ...), custom_call_target="tpu_custom_call" | custom-call | tf_op jit(solution)/shard_map/totals/pallas_call | solution.py:242
  3.6 17.5 %all_to_all.15.got_ref = bf16[4,144,128]{2,1,0:T(8,128)(2,1)S(1)} all-to-all(bf16[4,144,128]{2,1,0:T(8,128)(2,1)S(1)} %get-tuple-element.10), channel_id=1, replica_groups=mesh['samp'=8,'part'=4,'line'=4,'recv'=4] {'recv'}, dimensions={0} | all-to-all | bytes 294912 | tf_op jit(solution)/shard_map/all_to_all | solution.py:272
  21.0 0.3 tables.1
  21.4 13.5 %all_to_all.16.got_ref = bf16[16,48,128]{2,1,0:T(8,128)(2,1)S(1)} all-to-all(bf16[16,48,128]{2,1,0:T(8,128)(2,1)S(1)} %get-tuple-element.13), channel_id=1, replica_groups=mesh['samp'=8,'part'=4,'line'=4,'recv'=4] {'part','line'}, dimensions={0} | all-to-all | bytes 393216 | tf_op jit(solution)/shard_map/all_to_all | solution.py:283
  34.9 1.3 %product.1 = f32[16,1,128]{2,1,0:T(1,128)} custom-call(bf16[16,48,128]{2,1,0:T(8,128)(2,1)S(1)} %all_to_all.16.got_ref), custom_call_target="tpu_custom_call" | custom-call | tf_op jit(solution)/shard_map/product/pallas_call | solution.py:284
  36.2 5.1 %all-to-all-start.2 = ((f32[16,1,128]{2,1,0:T(1,128)}), f32[16,1,128]{2,1,0:T(1,128)S(1)}, u32[]{:S(2)}, u32[]{:S(2)}) async-start(f32[16,1,128]{2,1,0:T(1,128)} %product.1), calls=%async_computation.2 | async-start | bytes 16384 | tf_op jit(solution)/shard_map/all_to_all | solution.py:291
  41.3 3.0 %inverse.1.refs_1_ = f32[32,32]{1,0:T(8,128)S(1)} custom-call(bf16[16,48,128]{2,1,0:T(8,128)(2,1)S(1)} %all_to_all.16.got_ref, f32[32,32]{1,0:T(8,128)S(1)} %get-tuple-element.14.gram_ref), custom_call_target="tpu_custom_call" | custom-call | tf_op jit(solution)/shard_map/inverse/pallas_call | solution.py:292
  44.3 4.0 %all-to-all-done.2.refs_0_ = f32[16,1,128]{2,1,0:T(1,128)S(1)} async-done(((f32[16,1,128]{2,1,0:T(1,128)}), f32[16,1,128]{2,1,0:T(1,128)S(1)}, u32[]{:S(2)}, u32[]{:S(2)}) %all-to-all-start.2) | async-done | bytes 8224 | tf_op jit(solution)/shard_map/all_to_all | solution.py:291
  48.3 0.8 %apply.1 = f32[4,32]{1,0:T(4,128)} custom-call(f32[16,1,128]{2,1,0:T(1,128)S(1)} %all-to-all-done.2.refs_0_, f32[32,32]{1,0:T(8,128)S(1)} %inverse.1.refs_1_), custom_call_target="tpu_custom_call" | custom-call | tf_op jit(solution)/shard_map/apply/pallas_call | solution.py:299
Async XLA Ops:
  36.2 12.1 %all-to-all-start.2 = ((f32[16,1,128]{2,1,0:T(1,128)}), f32[16,1,128]{2,1,0:T(1,128)S(1)}, u32[]{:S(2)}, u32[]{:S(2)}) async-start(f32[16,1,128]{2,1,0:T(1,128)} %product.1), calls=%async_computation.2 | async-start | bytes 16384 | tf_op jit(solution)/shard_map/all_to_all | solution.py:291

commit v4 on v3

--- a/solution.py
+++ b/solution.py
@@ -97,26 +97,23 @@
 
 def fill_side(weight_ref, ligand_ref, receptor_ref, side_ref):
     rank = weight_ref.shape[0]
-    parts = rank // 8
     weight = weight_ref[...]
     gram = lax.dot_general(weight, weight, ROW_PAIRS, preferred_element_type=F32)
     terms = []
     for _ in range(3):
         term = gram.astype(BF16).astype(F32)
         gram = gram - term
-        terms += [term[8 * part : 8 * part + 8, 8 * part :] for part in range(parts)]
-    terms = jnp.concatenate(terms, axis=1)
-    terms = jnp.concatenate([terms, jnp.zeros((8, 2 * LANES - terms.shape[1]), F32)], axis=1)
-    ligand, receptor = ligand_ref[...], receptor_ref[...]
+        terms.append(term)
+    terms = jnp.concatenate(terms + [jnp.zeros((rank, LANES - 3 * rank), F32)], axis=1)
+    ligand, receptor = ligand_ref[...].astype(I32), receptor_ref[...].astype(I32)
     digits = [ligand >> 7, ligand & 127, receptor >> 7, receptor & 127]
-    place = iota((8, LANES), 0)
-    where = jnp.zeros((8, LANES), F32)
-    for spot, digit in enumerate(digits):
-        where = jnp.where(place == spot, digit.astype(F32), where)
+    digits = [digit.astype(F32) for digit in digits]
     weight = weight.astype(F32)
-    for part in range(parts):
-        pieces = [weight[8 * part : 8 * part + 8, :], where, terms[:, :LANES], terms[:, LANES:]]
-        side_ref[part] = jnp.concatenate(pieces, axis=0).astype(BF16)
+    for piece in range(rank // 2):
+        low = 8 * (2 * piece // 8)
+        rows = [terms[2 * piece : 2 * piece + 2, :], jnp.zeros((2, LANES), F32)]
+        rows = [weight[low : low + 8, :]] + digits + rows
+        side_ref[piece] = jnp.concatenate(rows, axis=0).astype(BF16)
 
 
 def tables_kernel(got_ref, sender_ref, side_ref, out_ref, gram_ref):
@@ -141,82 +138,89 @@
     receiver = jnp.concatenate(blocks, axis=1).astype(BF16)
     sender = sender_ref[...]
     tables = jnp.dot(jnp.concatenate([sender, receiver], axis=0), mean, preferred_element_type=F32)
+    own = lax.axis_index("recv")
+    lines = targets // parts
     for part in range(parts):
         low = part * 8
         both = [tables[low : low + 8, :], tables[rank + low : rank + low + 8, :]]
         both = jnp.concatenate(both, axis=0).astype(BF16)
-        side = side_ref[part]
-        for target in range(part * (targets // parts), (part + 1) * (targets // parts)):
-            out_ref[target, :16, :] = both
-            out_ref[target, 16:, :] = side
+        for line in range(lines):
+            out_ref[part * lines + line, :16, :] = both
+            out_ref[part * lines + line, 16:, :] = side_ref[part * 4 + (line + own) % 4]
     sender_gram = lax.dot_general(sender, sender, ROW_PAIRS, preferred_element_type=F32)
     receiver_gram = lax.dot_general(receiver, receiver, ROW_PAIRS, preferred_element_type=F32)
     gram_ref[...] = sender_gram * receiver_gram
 
 
-def product_kernel(got_ref, out_ref):
+def choose(values, which):
+    bit = 1
+    while len(values) > 1:
+        odd = (which & bit) != 0
+        values = [jnp.where(odd, b, a) for a, b in zip(values[::2], values[1::2])]
+        bit *= 2
+    return values[0]
+
+
+def product_kernel(rank, got_ref, out_ref):
     sources = got_ref.shape[0]
     tables = [got_ref[source, :16, :].astype(F32) for source in range(sources)]
     product = jnp.zeros((8, LANES), F32)
+    terms = jnp.zeros((8, LANES), F32)
     for source in range(sources):
         side = got_ref[source, 16:32, :].astype(F32)
+        terms = terms + side[8:, :]
         where = side[8:, :].astype(I32)
         digits = [jnp.broadcast_to(where[spot : spot + 1, :], (8, LANES)) for spot in range(4)]
-        ligand = jnp.zeros((8, LANES), F32)
-        receptor = jnp.zeros((8, LANES), F32)
-        for block in range(sources):
-            found = jnp.take_along_axis(tables[block][:8, :], digits[1], axis=1)
-            ligand = jnp.where(digits[0] == block, found, ligand)
-            found = jnp.take_along_axis(tables[block][8:, :], digits[3], axis=1)
-            receptor = jnp.where(digits[2] == block, found, receptor)
+        ligand = [jnp.take_along_axis(table[:8, :], digits[1], axis=1) for table in tables]
+        receptor = [jnp.take_along_axis(table[8:, :], digits[3], axis=1) for table in tables]
+        ligand, receptor = choose(ligand, digits[0]), choose(receptor, digits[2])
         product = product + ligand * receptor * side[:8, :]
     column = jnp.sum(product, axis=1, keepdims=True)
-    line = jnp.where(iota((8, LANES), 0) == iota((8, LANES), 1), column, 0.0)
-    line = jnp.sum(line, axis=0, keepdims=True)
+    rows, lanes = iota((8, LANES), 0), iota((8, LANES), 1)
+    own = lax.axis_index("recv")
+    spot = (lax.axis_index("line") + own) % 4
+    gram = terms[4:6, :rank] + terms[4:6, rank : 2 * rank] + terms[4:6, 2 * rank : 3 * rank]
+    gram = jnp.concatenate([gram, jnp.zeros((2, LANES - rank), F32)], axis=1)
+    gram = jnp.concatenate([gram] * 4, axis=0)
+    tile = jnp.where(rows >> 1 == spot, gram, 0.0)
+    tile = jnp.where(lanes == rank + own, column, tile)
     for target in range(out_ref.shape[0]):
-        out_ref[target] = line
-
-
-def inverse_kernel(got_ref, gram_ref, out_ref):
+        out_ref[target] = tile
+
+
+def solve_kernel(samples, got_ref, gram_ref, out_ref):
     rank = gram_ref.shape[0]
     parts = rank // 8
-    terms = jnp.sum(got_ref[:, 32:, :].astype(F32), axis=0)
-    terms = jnp.concatenate([terms[:8, :], terms[8:, :]], axis=1)
-    wide = sum(range(8, rank + 8, 8))
-    upper = terms[:, :wide] + terms[:, wide : 2 * wide] + terms[:, 2 * wide : 3 * wide]
-    lines, start = [], 0
+    scale = jnp.concatenate([gram_ref[...], jnp.ones((rank, LANES - rank), F32)], axis=1)
+    work = []
     for part in range(parts):
-        width = rank - 8 * part
-        line = upper[:, start : start + width]
-        if part:
-            line = jnp.concatenate([jnp.zeros((8, 8 * part), F32), line], axis=1)
-        lines.append(line)
-        start += width
-    upper = jnp.concatenate(lines, axis=0)
-    gram = jnp.where(iota((rank, rank), 0) <= iota((rank, rank), 1), upper, upper.T)
-    hadamard = gram * gram_ref[...]
-    rows = iota((rank, LANES), 0)
-    unit = jnp.where(iota((rank, LANES - rank), 0) == iota((rank, LANES - rank), 1), 1.0, 0.0)
-    work = jnp.concatenate([hadamard, unit], axis=1)
-    for j in range(rank):
-        pivot = work[j : j + 1, j : j + 1]
-        pivot = jnp.where(pivot > 0.0, pivot, jnp.nan)
-        line = work[j : j + 1, :] / pivot
-        work = jnp.where(rows == j, line, work - work[:, j : j + 1] * line)
-    out_ref[...] = work[:, rank : 2 * rank]
-
-
-def apply_kernel(samples, got_ref, inverse_ref, out_ref):
-    rank = inverse_ref.shape[0]
-    parts = got_ref.shape[0] // samples
-    lines = []
-    for sample in range(samples):
-        pieces = [got_ref[part * samples + sample, :, :8] for part in range(parts)]
-        lines.append(jnp.concatenate(pieces, axis=1))
-    product = jnp.concatenate(lines + [jnp.zeros((8 - samples, rank), F32)], axis=0)
-    answer = jnp.dot(
-        product, inverse_ref[...], precision=lax.Precision.HIGHEST, preferred_element_type=F32
-    )
+        block = got_ref[part * samples]
+        for sample in range(1, samples):
+            block = block + got_ref[part * samples + sample]
+        work.append(block * scale[8 * part : 8 * part + 8, :])
+    rows = iota((8, LANES), 0)
+    for part in range(parts):
+        columns = [
+            [jnp.broadcast_to(block[:, lane : lane + 1], (8, LANES)) for block in work]
+            for lane in range(8 * part, 8 * part + 8)
+        ]
+        lead, inner = work[part], [column[part] for column in columns]
+        for row in range(8):
+            pivot = inner[row][row : row + 1, :]
+            pivot = jnp.where(pivot > 0.0, 1.0 / pivot, jnp.nan)
+            here, times = rows == row, inner[row]
+            line = lead[row : row + 1, :] * pivot
+            lead = jnp.where(here, line, lead - times * line)
+            for later in range(row + 1, 8):
+                line = inner[later][row : row + 1, :] * pivot
+                inner[later] = jnp.where(here, line, inner[later] - times * line)
+        for other in range(parts):
+            if other == part:
+                work[other] = lead
+            else:
+                for row in range(8):
+                    work[other] = work[other] - columns[row][other] * lead[row : row + 1, :]
+    answer = jnp.concatenate(work, axis=0)[:, rank : rank + 8].T
     out_ref[...] = answer[:samples, :]
 
 
@@ -245,7 +249,7 @@
         out_specs=(vmem, vmem, vmem),
         out_shape=(
             pltpu.VMEM((samples, clusters + 16, genes), BF16),
-            pltpu.VMEM((rank // 8, 32, LANES), BF16),
+            pltpu.VMEM((rank // 2, 16, LANES), BF16),
             pltpu.VMEM((rank, clusters), BF16),
         ),
         scratch_shapes=[
@@ -275,34 +279,27 @@
         in_specs=[vmem] * 3,
         out_specs=(vmem, vmem),
         out_shape=(
-            pltpu.VMEM((targets, 48, genes), BF16),
+            pltpu.VMEM((targets, 32, genes), BF16),
             pltpu.VMEM((rank, rank), F32),
         ),
         name="tables",
     )(got, sender, side)
     got = on_chip(lax.all_to_all(sent, ("part", "line"), 0, 0, tiled=True))
     sent = pl.pallas_call(
-        product_kernel,
+        lambda *refs: product_kernel(rank, *refs),
         in_specs=[vmem],
         out_specs=vmem,
-        out_shape=pltpu.VMEM((parts * samples, 1, LANES), F32),
+        out_shape=pltpu.VMEM((parts * samples, 8, LANES), F32),
         name="product",
     )(got)
-    final = on_chip(lax.all_to_all(on_chip(sent), ("part", "recv"), 0, 0, tiled=True))
-    inverse = pl.pallas_call(
-        inverse_kernel,
-        in_specs=[vmem] * 2,
-        out_specs=vmem,
-        out_shape=pltpu.VMEM((rank, rank), F32),
-        name="inverse",
-    )(got, on_chip(gram))
+    got = on_chip(lax.all_to_all(sent, ("part", "recv"), 0, 0, tiled=True))
     return pl.pallas_call(
-        lambda *refs: apply_kernel(samples, *refs),
+        lambda *refs: solve_kernel(samples, *refs),
         in_specs=[vmem] * 2,
         out_specs=vmem,
         out_shape=jax.ShapeDtypeStruct((samples, rank), F32),
-        name="apply",
-    )(final, on_chip(inverse))
+        name="solve",
+    )(got, on_chip(gram))
 
 
 def solution(mesh):

time: 49.3 us -> 48.3 us (0.980)
  blocking collectives: 30.9 us -> 42.1 us
  starting transfers between devices: 5.14 us -> 0 us
  waiting for transfers between devices: 3.98 us -> 0 us
  Pallas kernels: 9.03 us -> 6.02 us
    all_to_all x0 -> x1, blocking collectives: none -> 12 us  [body(): got = on_chip(lax.all_to_all(sent, ('part', 'recv'), 0, 0, tiled=True))]
    all_to_all x1 -> x0, starting transfers between devices: 5.14 us -> none  [body(): lax.all_to_all(on_chip(sent), ('part', 'recv'), 0, 0, tiled=True)]
    all_to_all x1 -> x0, waiting for transfers between devices: 3.98 us -> none  [body(): lax.all_to_all(on_chip(sent), ('part', 'recv'), 0, 0, tiled=True)]
    pallas_call x3 -> x2, Pallas kernels: 5.12 us -> 2.1 us  [the longest x1 1.57 us: body(): pl.pallas_call(lambda *refs: solve_kernel(samples, *refs), in_specs=[vmem...]
    all_to_all x1, blocking collectives: 13.5 us -> 12.6 us  [body(): got = on_chip(lax.all_to_all(sent, ('part', 'line'), 0, 0, tiled=True))]
  transfers between devices with their start and end apart: 1 -> 0, of which waited for: 1 -> 0; matrix products, arithmetic and copies ran while one was open for 0% -> 0% of each run, Pallas kernels for 6% -> 0%
where the time goes in v4:
time: 48.3 us; the launch traced here: 48.1 us
  blocking collectives  42.1 us (87%)
  Pallas kernels  6.02 us (12%)
    all_to_all x1, blocking collectives, body(): got = on_chip(lax.all_to_all(sums, 'recv', 0, 0, tiled=True))  17.5 us
    all_to_all x1, blocking collectives, body(): got = on_chip(lax.all_to_all(sent, ('part', 'line'), 0, 0, tiled=True))  12.6 us
    all_to_all x1, blocking collectives, body(): got = on_chip(lax.all_to_all(sent, ('part', 'recv'), 0, 0, tiled=True))  12 us
    pallas_call x1, Pallas kernels, body(): pl.pallas_call(totals_kernel, in_specs=[anywhere] * 7, out_specs=(vmem, v...  3.58 us
    pallas_call x1, Pallas kernels, body(): pl.pallas_call(lambda *refs: solve_kernel(samples, *refs), in_specs=[vmem...  1.57 us

profile of v4, /device:TPU:1, one launch (start us, length us, event | category | flops | bytes accessed | tf_op | source)
XLA Modules:
  0.0 48.1 jit_solution(4630803704544593887)
XLA Ops:
  0.0 3.6 %totals.1 = (bf16[4,144,128]{2,1,0:T(8,128)(2,1)S(1)}, bf16[16,16,128]{2,1,0:T(8,128)(2,1)S(1)}, bf16[32,128]{1,0:T(8,128)(2,1)S(1)}) custom-call(bf16[4,4096,128]{2,1,0:T(8,128)(2,1)} %x_hbm.1, s32[4,4096]{1,0:T(4,128)} %labels_hbm.1, bf16[32,32]{1,0:T(8,128)(2,1)} %receiver_hbm.1, bf16[32,128]{1,0:T(8,128)(2,1)} %bitcast.4, bf16[32,128]{1,0:T(8,128)(2,1)} %bitcast.5, ...), custom_call_target="tpu_custom_call" | custom-call | tf_op jit(solution)/shard_map/totals/pallas_call | solution.py:246
  3.6 17.5 %all_to_all.15.got_ref = bf16[4,144,128]{2,1,0:T(8,128)(2,1)S(1)} all-to-all(bf16[4,144,128]{2,1,0:T(8,128)(2,1)S(1)} %get-tuple-element.10), channel_id=1, replica_groups=mesh['samp'=8,'part'=4,'line'=4,'recv'=4] {'recv'}, dimensions={0} | all-to-all | bytes 294912 | tf_op jit(solution)/shard_map/all_to_all | solution.py:276
  21.0 0.3 tables.1
  21.4 12.6 %all_to_all.16.refs_0_ = bf16[16,32,128]{2,1,0:T(8,128)(2,1)S(1)} all-to-all(bf16[16,32,128]{2,1,0:T(8,128)(2,1)S(1)} %get-tuple-element.13), channel_id=1, replica_groups=mesh['samp'=8,'part'=4,'line'=4,'recv'=4] {'part','line'}, dimensions={0} | all-to-all | bytes 262144 | tf_op jit(solution)/shard_map/all_to_all | solution.py:287
  34.0 0.5 %product.1 = f32[16,8,128]{2,1,0:T(8,128)S(1)} custom-call(bf16[16,32,128]{2,1,0:T(8,128)(2,1)S(1)} %all_to_all.16.refs_0_), custom_call_target="tpu_custom_call" | custom-call | tf_op jit(solution)/shard_map/product/pallas_call | solution.py:288
  34.5 12.0 %all_to_all.17.refs_0_ = f32[16,8,128]{2,1,0:T(8,128)S(1)} all-to-all(f32[16,8,128]{2,1,0:T(8,128)S(1)} %product.1), channel_id=1, replica_groups=mesh['samp'=8,'part'=4,'line'=4,'recv'=4] {'part','recv'}, dimensions={0} | all-to-all | bytes 131072 | tf_op jit(solution)/shard_map/all_to_all | solution.py:295
  46.5 1.6 %solve.1 = f32[4,32]{1,0:T(4,128)} custom-call(f32[16,8,128]{2,1,0:T(8,128)S(1)} %all_to_all.17.refs_0_, f32[32,32]{1,0:T(8,128)S(1)} %get-tuple-element.14.refs_1_), custom_call_target="tpu_custom_call" | custom-call | tf_op jit(solution)/shard_map/solve/pallas_call | solution.py:296

commit v5 on v4

--- a/solution.py
+++ b/solution.py
@@ -38,21 +38,23 @@
             ]
         )
     ]
-    small[0].start()
-    halves = [(0, samples // 2), (samples // 2, samples)]
+    for copy in small:
+        copy.start()
+    spans = [(sample, sample + 1) for sample in range(samples)]
     large = [
         pltpu.make_async_copy(x_hbm.at[pl.ds(a, b - a)], x_ref.at[pl.ds(a, b - a)], x_sem.at[i])
-        for i, (a, b) in enumerate(halves)
+        for i, (a, b) in enumerate(spans)
     ]
-    for copy in large:
-        copy.start()
-    for copy in small[1:]:
-        copy.start()
+    for spot, copy in enumerate(large):
+        copy.start(priority=min(spot, 1))
     small[0].wait()
     kinds = iota((clusters, CHUNK), 0).astype(F32).astype(BF16)
     one, zero = jnp.ones((), BF16), jnp.zeros((), BF16)
+    for other in small[1:]:
+        other.wait()
+    fill_side(weight_ref, ligand_ref, receptor_ref, side_ref)
     extras = {}
-    for (first, last), copy in zip(halves, large):
+    for (first, last), copy in zip(spans, large):
         members, counts = {}, {}
         for sample in range(first, last):
             count = jnp.zeros((clusters, LANES), BF16)
@@ -72,10 +74,6 @@
             counts[sample] = jnp.dot(
                 count, jnp.ones((LANES, genes), BF16), preferred_element_type=F32
             )
-        if first:
-            for other in small[1:]:
-                other.wait()
-            fill_side(weight_ref, ligand_ref, receptor_ref, side_ref)
         copy.wait()
         for sample in range(first, last):
             total = jnp.zeros((clusters, genes), F32)
@@ -259,7 +257,7 @@
             pltpu.VMEM((rank, LANES), BF16),
             pltpu.VMEM((1, LANES), I32),
             pltpu.VMEM((1, LANES), I32),
-            pltpu.SemaphoreType.DMA((2,)),
+            pltpu.SemaphoreType.DMA((samples,)),
             pltpu.SemaphoreType.DMA((6,)),
         ],
         name="totals",

time: 48.3 us -> 48 us (level)
  no operation moved by 1% of the time
where the time goes in v5:
time: 48 us; the launch traced here: 47.8 us
  blocking collectives  42.1 us (88%)
  Pallas kernels  5.75 us (12%)
    all_to_all x1, blocking collectives, body(): got = on_chip(lax.all_to_all(sums, 'recv', 0, 0, tiled=True))  17.5 us
    all_to_all x1, blocking collectives, body(): got = on_chip(lax.all_to_all(sent, ('part', 'line'), 0, 0, tiled=True))  12.6 us
    all_to_all x1, blocking collectives, body(): got = on_chip(lax.all_to_all(sent, ('part', 'recv'), 0, 0, tiled=True))  12 us
    pallas_call x1, Pallas kernels, body(): pl.pallas_call(totals_kernel, in_specs=[anywhere] * 7, out_specs=(vmem, v...  3.31 us
    pallas_call x1, Pallas kernels, body(): pl.pallas_call(lambda *refs: solve_kernel(samples, *refs), in_specs=[vmem...  1.57 us

profile of v5, /device:TPU:1, one launch (start us, length us, event | category | flops | bytes accessed | tf_op | source)
XLA Modules:
  0.0 47.8 jit_solution(12991023575070632637)
XLA Ops:
  0.0 3.3 %totals.1 = (bf16[4,144,128]{2,1,0:T(8,128)(2,1)S(1)}, bf16[16,16,128]{2,1,0:T(8,128)(2,1)S(1)}, bf16[32,128]{1,0:T(8,128)(2,1)S(1)}) custom-call(bf16[4,4096,128]{2,1,0:T(8,128)(2,1)} %x_hbm.1, s32[4,4096]{1,0:T(4,128)} %labels_hbm.1, bf16[32,32]{1,0:T(8,128)(2,1)} %receiver_hbm.1, bf16[32,128]{1,0:T(8,128)(2,1)} %bitcast.4, bf16[32,128]{1,0:T(8,128)(2,1)} %bitcast.5, ...), custom_call_target="tpu_custom_call" | custom-call | tf_op jit(solution)/shard_map/totals/pallas_call | solution.py:244
  3.3 17.5 %all_to_all.15.got_ref = bf16[4,144,128]{2,1,0:T(8,128)(2,1)S(1)} all-to-all(bf16[4,144,128]{2,1,0:T(8,128)(2,1)S(1)} %get-tuple-element.10), channel_id=1, replica_groups=mesh['samp'=8,'part'=4,'line'=4,'recv'=4] {'recv'}, dimensions={0} | all-to-all | bytes 294912 | tf_op jit(solution)/shard_map/all_to_all | solution.py:274
  20.8 0.3 tables.1
  21.1 12.6 %all_to_all.16.refs_0_ = bf16[16,32,128]{2,1,0:T(8,128)(2,1)S(1)} all-to-all(bf16[16,32,128]{2,1,0:T(8,128)(2,1)S(1)} %get-tuple-element.13), channel_id=1, replica_groups=mesh['samp'=8,'part'=4,'line'=4,'recv'=4] {'part','line'}, dimensions={0} | all-to-all | bytes 262144 | tf_op jit(solution)/shard_map/all_to_all | solution.py:285
  33.7 0.5 %product.1 = f32[16,8,128]{2,1,0:T(8,128)S(1)} custom-call(bf16[16,32,128]{2,1,0:T(8,128)(2,1)S(1)} %all_to_all.16.refs_0_), custom_call_target="tpu_custom_call" | custom-call | tf_op jit(solution)/shard_map/product/pallas_call | solution.py:286
  34.2 12.0 %all_to_all.17.refs_0_ = f32[16,8,128]{2,1,0:T(8,128)S(1)} all-to-all(f32[16,8,128]{2,1,0:T(8,128)S(1)} %product.1), channel_id=1, replica_groups=mesh['samp'=8,'part'=4,'line'=4,'recv'=4] {'part','recv'}, dimensions={0} | all-to-all | bytes 131072 | tf_op jit(solution)/shard_map/all_to_all | solution.py:293
  46.2 1.6 %solve.1 = f32[4,32]{1,0:T(4,128)} custom-call(f32[16,8,128]{2,1,0:T(8,128)S(1)} %all_to_all.17.refs_0_, f32[32,32]{1,0:T(8,128)S(1)} %get-tuple-element.14.refs_1_), custom_call_target="tpu_custom_call" | custom-call | tf_op jit(solution)/shard_map/solve/pallas_call | solution.py:294

commit v6 on v5

--- a/solution.py
+++ b/solution.py
@@ -143,8 +143,8 @@
         both = [tables[low : low + 8, :], tables[rank + low : rank + low + 8, :]]
         both = jnp.concatenate(both, axis=0).astype(BF16)
         for line in range(lines):
-            out_ref[part * lines + line, :16, :] = both
-            out_ref[part * lines + line, 16:, :] = side_ref[part * 4 + (line + own) % 4]
+            out_ref[line * parts + part, :16, :] = both
+            out_ref[line * parts + part, 16:, :] = side_ref[part * 4 + (line + own) % 4]
     sender_gram = lax.dot_general(sender, sender, ROW_PAIRS, preferred_element_type=F32)
     receiver_gram = lax.dot_general(receiver, receiver, ROW_PAIRS, preferred_element_type=F32)
     gram_ref[...] = sender_gram * receiver_gram
@@ -161,7 +161,8 @@
 
 def product_kernel(rank, got_ref, out_ref):
     sources = got_ref.shape[0]
-    tables = [got_ref[source, :16, :].astype(F32) for source in range(sources)]
+    order = [line * 4 + part for part in range(4) for line in range(sources // 4)]
+    tables = [got_ref[source, :16, :].astype(F32) for source in order]
     product = jnp.zeros((8, LANES), F32)
     terms = jnp.zeros((8, LANES), F32)
     for source in range(sources):
@@ -282,7 +283,7 @@
         ),
         name="tables",
     )(got, sender, side)
-    got = on_chip(lax.all_to_all(sent, ("part", "line"), 0, 0, tiled=True))
+    got = on_chip(lax.all_to_all(sent, ("line", "part"), 0, 0, tiled=True))
     sent = pl.pallas_call(
         lambda *refs: product_kernel(rank, *refs),
         in_specs=[vmem],

time: 48 us -> 47.5 us (0.990)
  blocking collectives: 42.1 us -> 41.5 us
    all_to_all x1, blocking collectives: 12.6 us -> 12 us  [body(): got = on_chip(lax.all_to_all(sent, ('line', 'part'), 0, 0, tiled=True))]
where the time goes in v6:
time: 47.5 us; the launch traced here: 47.3 us
  blocking collectives  41.5 us (87%)
  Pallas kernels  5.75 us (12%)
    all_to_all x1, blocking collectives, body(): got = on_chip(lax.all_to_all(sums, 'recv', 0, 0, tiled=True))  17.5 us
    all_to_all x1, blocking collectives, body(): got = on_chip(lax.all_to_all(sent, ('line', 'part'), 0, 0, tiled=True))  12 us
    all_to_all x1, blocking collectives, body(): got = on_chip(lax.all_to_all(sent, ('part', 'recv'), 0, 0, tiled=True))  12 us
    pallas_call x1, Pallas kernels, body(): pl.pallas_call(totals_kernel, in_specs=[anywhere] * 7, out_specs=(vmem, v...  3.31 us
    pallas_call x1, Pallas kernels, body(): pl.pallas_call(lambda *refs: solve_kernel(samples, *refs), in_specs=[vmem...  1.57 us

profile of v6, /device:TPU:1, one launch (start us, length us, event | category | flops | bytes accessed | tf_op | source)
XLA Modules:
  0.0 47.3 jit_solution(13809846175771949557)
XLA Ops:
  0.0 3.3 %totals.1 = (bf16[4,144,128]{2,1,0:T(8,128)(2,1)S(1)}, bf16[16,16,128]{2,1,0:T(8,128)(2,1)S(1)}, bf16[32,128]{1,0:T(8,128)(2,1)S(1)}) custom-call(bf16[4,4096,128]{2,1,0:T(8,128)(2,1)} %x_hbm.1, s32[4,4096]{1,0:T(4,128)} %labels_hbm.1, bf16[32,32]{1,0:T(8,128)(2,1)} %receiver_hbm.1, bf16[32,128]{1,0:T(8,128)(2,1)} %bitcast.4, bf16[32,128]{1,0:T(8,128)(2,1)} %bitcast.5, ...), custom_call_target="tpu_custom_call" | custom-call | tf_op jit(solution)/shard_map/totals/pallas_call | solution.py:245
  3.3 17.5 %all_to_all.15.got_ref = bf16[4,144,128]{2,1,0:T(8,128)(2,1)S(1)} all-to-all(bf16[4,144,128]{2,1,0:T(8,128)(2,1)S(1)} %get-tuple-element.10), channel_id=1, replica_groups=mesh['samp'=8,'part'=4,'line'=4,'recv'=4] {'recv'}, dimensions={0} | all-to-all | bytes 294912 | tf_op jit(solution)/shard_map/all_to_all | solution.py:275
  20.8 0.3 tables.1
  21.1 12.0 %all_to_all.16.refs_0_ = bf16[16,32,128]{2,1,0:T(8,128)(2,1)S(1)} all-to-all(bf16[16,32,128]{2,1,0:T(8,128)(2,1)S(1)} %get-tuple-element.13), channel_id=1, replica_groups=mesh['samp'=8,'part'=4,'line'=4,'recv'=4] {'line','part'}, dimensions={0} | all-to-all | bytes 262144 | tf_op jit(solution)/shard_map/all_to_all | solution.py:286
  33.2 0.5 %product.1 = f32[16,8,128]{2,1,0:T(8,128)S(1)} custom-call(bf16[16,32,128]{2,1,0:T(8,128)(2,1)S(1)} %all_to_all.16.refs_0_), custom_call_target="tpu_custom_call" | custom-call | tf_op jit(solution)/shard_map/product/pallas_call | solution.py:287
  33.7 12.0 %all_to_all.17.refs_0_ = f32[16,8,128]{2,1,0:T(8,128)S(1)} all-to-all(f32[16,8,128]{2,1,0:T(8,128)S(1)} %product.1), channel_id=1, replica_groups=mesh['samp'=8,'part'=4,'line'=4,'recv'=4] {'part','recv'}, dimensions={0} | all-to-all | bytes 131072 | tf_op jit(solution)/shard_map/all_to_all | solution.py:294
  45.7 1.6 %solve.1 = f32[4,32]{1,0:T(4,128)} custom-call(f32[16,8,128]{2,1,0:T(8,128)S(1)} %all_to_all.17.refs_0_, f32[32,32]{1,0:T(8,128)S(1)} %get-tuple-element.14.refs_1_), custom_call_target="tpu_custom_call" | custom-call | tf_op jit(solution)/shard_map/solve/pallas_call | solution.py:295

commit v7 on v6

--- a/solution.py
+++ b/solution.py
@@ -175,29 +175,34 @@
         ligand, receptor = choose(ligand, digits[0]), choose(receptor, digits[2])
         product = product + ligand * receptor * side[:8, :]
     column = jnp.sum(product, axis=1, keepdims=True)
-    rows, lanes = iota((8, LANES), 0), iota((8, LANES), 1)
-    own = lax.axis_index("recv")
-    spot = (lax.axis_index("line") + own) % 4
+    line = jnp.where(iota((8, LANES), 1) == iota((8, LANES), 0) + 2 * rank, column, 0.0)
+    line = jnp.sum(line, axis=0, keepdims=True)
     gram = terms[4:6, :rank] + terms[4:6, rank : 2 * rank] + terms[4:6, 2 * rank : 3 * rank]
-    gram = jnp.concatenate([gram, jnp.zeros((2, LANES - rank), F32)], axis=1)
-    gram = jnp.concatenate([gram] * 4, axis=0)
-    tile = jnp.where(rows >> 1 == spot, gram, 0.0)
-    tile = jnp.where(lanes == rank + own, column, tile)
+    gram = [gram[:1, :], gram[1:, :], jnp.zeros((1, LANES - 2 * rank), F32)]
+    line = line + jnp.concatenate(gram, axis=1)
     for target in range(out_ref.shape[0]):
-        out_ref[target] = tile
+        out_ref[target] = line
 
 
 def solve_kernel(samples, got_ref, gram_ref, out_ref):
     rank = gram_ref.shape[0]
     parts = rank // 8
     scale = jnp.concatenate([gram_ref[...], jnp.ones((rank, LANES - rank), F32)], axis=1)
+    rows, lanes = iota((8, LANES), 0), iota((8, LANES), 1)
+    here = lax.axis_index("line")
     work = []
     for part in range(parts):
-        block = got_ref[part * samples]
-        for sample in range(1, samples):
-            block = block + got_ref[part * samples + sample]
+        block = jnp.zeros((8, LANES), F32)
+        for sample in range(samples):
+            line = got_ref[part * samples + sample]
+            second = jnp.concatenate([line[:, rank:], line[:, :rank]], axis=1)
+            both = jnp.where((rows & 1) == 0, line, second)
+            piece = ((rows >> 1) == (here + sample) % 4) & (lanes < rank)
+            block = jnp.where(piece, both, block)
+            column = jnp.where(lanes == rows + 2 * rank, line, 0.0)
+            column = jnp.sum(column, axis=1, keepdims=True)
+            block = jnp.where(lanes == rank + sample, column, block)
         work.append(block * scale[8 * part : 8 * part + 8, :])
-    rows = iota((8, LANES), 0)
     for part in range(parts):
         columns = [
             [jnp.broadcast_to(block[:, lane : lane + 1], (8, LANES)) for block in work]
@@ -288,7 +293,7 @@
         lambda *refs: product_kernel(rank, *refs),
         in_specs=[vmem],
         out_specs=vmem,
-        out_shape=pltpu.VMEM((parts * samples, 8, LANES), F32),
+        out_shape=pltpu.VMEM((parts * samples, 1, LANES), F32),
         name="product",
     )(got)
     got = on_chip(lax.all_to_all(sent, ("part", "recv"), 0, 0, tiled=True))

time: 47.5 us -> 47.1 us (level)
  blocking collectives: 41.5 us -> 40.8 us
    all_to_all x1, blocking collectives: 12 us -> 11.3 us  [body(): got = on_chip(lax.all_to_all(sent, ('part', 'recv'), 0, 0, tiled=True))]
where the time goes in v7:
time: 47.1 us; the launch traced here: 46.9 us
  blocking collectives  40.8 us (87%)
  Pallas kernels  6.04 us (13%)
    all_to_all x1, blocking collectives, body(): got = on_chip(lax.all_to_all(sums, 'recv', 0, 0, tiled=True))  17.5 us
    all_to_all x1, blocking collectives, body(): got = on_chip(lax.all_to_all(sent, ('line', 'part'), 0, 0, tiled=True))  12 us
    all_to_all x1, blocking collectives, body(): got = on_chip(lax.all_to_all(sent, ('part', 'recv'), 0, 0, tiled=True))  11.3 us
    pallas_call x1, Pallas kernels, body(): pl.pallas_call(totals_kernel, in_specs=[anywhere] * 7, out_specs=(vmem, v...  3.31 us
    pallas_call x1, Pallas kernels, body(): pl.pallas_call(lambda *refs: solve_kernel(samples, *refs), in_specs=[vmem...  1.85 us

profile of v7, /device:TPU:1, one launch (start us, length us, event | category | flops | bytes accessed | tf_op | source)
XLA Modules:
  0.0 46.9 jit_solution(521892037206374079)
XLA Ops:
  0.0 3.3 %totals.1 = (bf16[4,144,128]{2,1,0:T(8,128)(2,1)S(1)}, bf16[16,16,128]{2,1,0:T(8,128)(2,1)S(1)}, bf16[32,128]{1,0:T(8,128)(2,1)S(1)}) custom-call(bf16[4,4096,128]{2,1,0:T(8,128)(2,1)} %x_hbm.1, s32[4,4096]{1,0:T(4,128)} %labels_hbm.1, bf16[32,32]{1,0:T(8,128)(2,1)} %receiver_hbm.1, bf16[32,128]{1,0:T(8,128)(2,1)} %bitcast.4, bf16[32,128]{1,0:T(8,128)(2,1)} %bitcast.5, ...), custom_call_target="tpu_custom_call" | custom-call | tf_op jit(solution)/shard_map/totals/pallas_call | solution.py:250
  3.3 17.5 %all_to_all.15.got_ref = bf16[4,144,128]{2,1,0:T(8,128)(2,1)S(1)} all-to-all(bf16[4,144,128]{2,1,0:T(8,128)(2,1)S(1)} %get-tuple-element.10), channel_id=1, replica_groups=mesh['samp'=8,'part'=4,'line'=4,'recv'=4] {'recv'}, dimensions={0} | all-to-all | bytes 294912 | tf_op jit(solution)/shard_map/all_to_all | solution.py:280
  20.8 0.3 tables.1
  21.1 12.0 %all_to_all.16.refs_0_ = bf16[16,32,128]{2,1,0:T(8,128)(2,1)S(1)} all-to-all(bf16[16,32,128]{2,1,0:T(8,128)(2,1)S(1)} %get-tuple-element.13), channel_id=1, replica_groups=mesh['samp'=8,'part'=4,'line'=4,'recv'=4] {'line','part'}, dimensions={0} | all-to-all | bytes 262144 | tf_op jit(solution)/shard_map/all_to_all | solution.py:291
  33.2 0.5 %product.1 = f32[16,1,128]{2,1,0:T(1,128)S(1)} custom-call(bf16[16,32,128]{2,1,0:T(8,128)(2,1)S(1)} %all_to_all.16.refs_0_), custom_call_target="tpu_custom_call" | custom-call | tf_op jit(solution)/shard_map/product/pallas_call | solution.py:292
  33.7 11.3 %all_to_all.17.refs_0_ = f32[16,1,128]{2,1,0:T(1,128)S(1)} all-to-all(f32[16,1,128]{2,1,0:T(1,128)S(1)} %product.1), channel_id=1, replica_groups=mesh['samp'=8,'part'=4,'line'=4,'recv'=4] {'part','recv'}, dimensions={0} | all-to-all | bytes 16384 | tf_op jit(solution)/shard_map/all_to_all | solution.py:299
  45.0 1.9 %solve.1 = f32[4,32]{1,0:T(4,128)} custom-call(f32[16,1,128]{2,1,0:T(1,128)S(1)} %all_to_all.17.refs_0_, f32[32,32]{1,0:T(8,128)S(1)} %get-tuple-element.14.refs_1_), custom_call_target="tpu_custom_call" | custom-call | tf_op jit(solution)/shard_map/solve/pallas_call | solution.py:300

commit v8 on v7

--- a/solution.py
+++ b/solution.py
@@ -184,31 +184,40 @@
         out_ref[target] = line
 
 
+def total_of(terms):
+    while len(terms) > 1:
+        rest = terms[len(terms) // 2 * 2 :]
+        terms = [a + b for a, b in zip(terms[::2], terms[1::2])] + rest
+    return terms[0]
+
+
 def solve_kernel(samples, got_ref, gram_ref, out_ref):
     rank = gram_ref.shape[0]
     parts = rank // 8
     scale = jnp.concatenate([gram_ref[...], jnp.ones((rank, LANES - rank), F32)], axis=1)
-    rows, lanes = iota((8, LANES), 0), iota((8, LANES), 1)
-    here = lax.axis_index("line")
+    rows = iota((8, LANES), 0)
+    line = lax.axis_index("line")
+    first = jnp.concatenate([got_ref[source] for source in range(parts * samples)], axis=0)
+    second = jnp.concatenate([first[:, rank:], first[:, :rank]], axis=1)
+    right = first.T[2 * rank : 2 * rank + 8, :]
     work = []
     for part in range(parts):
-        block = jnp.zeros((8, LANES), F32)
+        low = part * samples
+        block = jnp.zeros((8, rank), F32)
         for sample in range(samples):
-            line = got_ref[part * samples + sample]
-            second = jnp.concatenate([line[:, rank:], line[:, :rank]], axis=1)
-            both = jnp.where((rows & 1) == 0, line, second)
-            piece = ((rows >> 1) == (here + sample) % 4) & (lanes < rank)
-            block = jnp.where(piece, both, block)
-            column = jnp.where(lanes == rows + 2 * rank, line, 0.0)
-            column = jnp.sum(column, axis=1, keepdims=True)
-            block = jnp.where(lanes == rank + sample, column, block)
+            at = low + sample
+            both = jnp.where((rows & 1) == 0, first[at : at + 1, :], second[at : at + 1, :])
+            piece = (rows >> 1)[:, :rank] == (line + sample) % 4
+            block = jnp.where(piece, both[:, :rank], block)
+        rest = jnp.zeros((8, LANES - rank - samples), F32)
+        block = jnp.concatenate([block, right[:, low : low + samples], rest], axis=1)
         work.append(block * scale[8 * part : 8 * part + 8, :])
     for part in range(parts):
-        columns = [
-            [jnp.broadcast_to(block[:, lane : lane + 1], (8, LANES)) for block in work]
+        spread = [
+            [jnp.broadcast_to(block[:, lane : lane + 1], (8, LANES)) for block in work[part:]]
             for lane in range(8 * part, 8 * part + 8)
         ]
-        lead, inner = work[part], [column[part] for column in columns]
+        lead, inner = work[part], [column[0] for column in spread]
         for row in range(8):
             pivot = inner[row][row : row + 1, :]
             pivot = jnp.where(pivot > 0.0, 1.0 / pivot, jnp.nan)
@@ -218,12 +227,17 @@
             for later in range(row + 1, 8):
                 line = inner[later][row : row + 1, :] * pivot
                 inner[later] = jnp.where(here, line, inner[later] - times * line)
-        for other in range(parts):
-            if other == part:
-                work[other] = lead
-            else:
-                for row in range(8):
-                    work[other] = work[other] - columns[row][other] * lead[row : row + 1, :]
+        work[part] = lead
+        for other in range(part + 1, parts):
+            terms = [spread[row][other - part] * lead[row : row + 1, :] for row in range(8)]
+            work[other] = work[other] - total_of(terms)
+    for part in range(parts - 2, -1, -1):
+        terms = [
+            jnp.broadcast_to(work[part][:, lane : lane + 1], (8, LANES))
+            * work[lane // 8][lane % 8 : lane % 8 + 1, :]
+            for lane in range(8 * part + 8, rank)
+        ]
+        work[part] = work[part] - total_of(terms)
     answer = jnp.concatenate(work, axis=0)[:, rank : rank + 8].T
     out_ref[...] = answer[:samples, :]
 

time: 47.1 us -> 46.9 us (level)
  no operation moved by 1% of the time
where the time goes in v8:
time: 46.9 us; the launch traced here: 46.7 us
  blocking collectives  40.8 us (87%)
  Pallas kernels  5.86 us (12%)
    all_to_all x1, blocking collectives, body(): got = on_chip(lax.all_to_all(sums, 'recv', 0, 0, tiled=True))  17.5 us
    all_to_all x1, blocking collectives, body(): got = on_chip(lax.all_to_all(sent, ('line', 'part'), 0, 0, tiled=True))  12 us
    all_to_all x1, blocking collectives, body(): got = on_chip(lax.all_to_all(sent, ('part', 'recv'), 0, 0, tiled=True))  11.3 us
    pallas_call x1, Pallas kernels, body(): pl.pallas_call(totals_kernel, in_specs=[anywhere] * 7, out_specs=(vmem, v...  3.31 us
    pallas_call x1, Pallas kernels, body(): pl.pallas_call(lambda *refs: solve_kernel(samples, *refs), in_specs=[vmem...  1.67 us

profile of v8, /device:TPU:1, one launch (start us, length us, event | category | flops | bytes accessed | tf_op | source)
XLA Modules:
  0.0 46.7 jit_solution(8014490442255693176)
XLA Ops:
  0.0 3.3 %totals.1 = (bf16[4,144,128]{2,1,0:T(8,128)(2,1)S(1)}, bf16[16,16,128]{2,1,0:T(8,128)(2,1)S(1)}, bf16[32,128]{1,0:T(8,128)(2,1)S(1)}) custom-call(bf16[4,4096,128]{2,1,0:T(8,128)(2,1)} %x_hbm.1, s32[4,4096]{1,0:T(4,128)} %labels_hbm.1, bf16[32,32]{1,0:T(8,128)(2,1)} %receiver_hbm.1, bf16[32,128]{1,0:T(8,128)(2,1)} %bitcast.4, bf16[32,128]{1,0:T(8,128)(2,1)} %bitcast.5, ...), custom_call_target="tpu_custom_call" | custom-call | tf_op jit(solution)/shard_map/totals/pallas_call | solution.py:264
  3.3 17.5 %all_to_all.15.got_ref = bf16[4,144,128]{2,1,0:T(8,128)(2,1)S(1)} all-to-all(bf16[4,144,128]{2,1,0:T(8,128)(2,1)S(1)} %get-tuple-element.10), channel_id=1, replica_groups=mesh['samp'=8,'part'=4,'line'=4,'recv'=4] {'recv'}, dimensions={0} | all-to-all | bytes 294912 | tf_op jit(solution)/shard_map/all_to_all | solution.py:294
  20.8 0.3 tables.1
  21.1 12.0 %all_to_all.16.refs_0_ = bf16[16,32,128]{2,1,0:T(8,128)(2,1)S(1)} all-to-all(bf16[16,32,128]{2,1,0:T(8,128)(2,1)S(1)} %get-tuple-element.13), channel_id=1, replica_groups=mesh['samp'=8,'part'=4,'line'=4,'recv'=4] {'line','part'}, dimensions={0} | all-to-all | bytes 262144 | tf_op jit(solution)/shard_map/all_to_all | solution.py:305
  33.2 0.5 %product.1 = f32[16,1,128]{2,1,0:T(1,128)S(1)} custom-call(bf16[16,32,128]{2,1,0:T(8,128)(2,1)S(1)} %all_to_all.16.refs_0_), custom_call_target="tpu_custom_call" | custom-call | tf_op jit(solution)/shard_map/product/pallas_call | solution.py:306
  33.7 11.3 %all_to_all.17.refs_0_ = f32[16,1,128]{2,1,0:T(1,128)S(1)} all-to-all(f32[16,1,128]{2,1,0:T(1,128)S(1)} %product.1), channel_id=1, replica_groups=mesh['samp'=8,'part'=4,'line'=4,'recv'=4] {'part','recv'}, dimensions={0} | all-to-all | bytes 16384 | tf_op jit(solution)/shard_map/all_to_all | solution.py:313
  45.0 1.7 %solve.1 = f32[4,32]{1,0:T(4,128)} custom-call(f32[16,1,128]{2,1,0:T(1,128)S(1)} %all_to_all.17.refs_0_, f32[32,32]{1,0:T(8,128)S(1)} %get-tuple-element.14.refs_1_), custom_call_target="tpu_custom_call" | custom-call | tf_op jit(solution)/shard_map/solve/pallas_call | solution.py:314

commit v9 on v8

--- a/solution.py
+++ b/solution.py
@@ -46,7 +46,7 @@
         for i, (a, b) in enumerate(spans)
     ]
     for spot, copy in enumerate(large):
-        copy.start(priority=min(spot, 1))
+        copy.start(priority=min(spot // 2, 1))
     small[0].wait()
     kinds = iota((clusters, CHUNK), 0).astype(F32).astype(BF16)
     one, zero = jnp.ones((), BF16), jnp.zeros((), BF16)

time: 46.9 us -> 47.2 us (level)
  no operation moved by 1% of the time
where the time goes in v9:
time: 47.2 us; the launch traced here: 47 us
  blocking collectives  40.8 us (86%)
  Pallas kernels  6.16 us (13%)
    all_to_all x1, blocking collectives, body(): got = on_chip(lax.all_to_all(sums, 'recv', 0, 0, tiled=True))  17.5 us
    all_to_all x1, blocking collectives, body(): got = on_chip(lax.all_to_all(sent, ('line', 'part'), 0, 0, tiled=True))  12 us
    all_to_all x1, blocking collectives, body(): got = on_chip(lax.all_to_all(sent, ('part', 'recv'), 0, 0, tiled=True))  11.3 us
    pallas_call x1, Pallas kernels, body(): pl.pallas_call(totals_kernel, in_specs=[anywhere] * 7, out_specs=(vmem, v...  3.62 us
    pallas_call x1, Pallas kernels, body(): pl.pallas_call(lambda *refs: solve_kernel(samples, *refs), in_specs=[vmem...  1.67 us

profile of v9, /device:TPU:1, one launch (start us, length us, event | category | flops | bytes accessed | tf_op | source)
XLA Modules:
  0.0 47.0 jit_solution(7073696875963693533)
XLA Ops:
  0.0 3.6 %totals.1 = (bf16[4,144,128]{2,1,0:T(8,128)(2,1)S(1)}, bf16[16,16,128]{2,1,0:T(8,128)(2,1)S(1)}, bf16[32,128]{1,0:T(8,128)(2,1)S(1)}) custom-call(bf16[4,4096,128]{2,1,0:T(8,128)(2,1)} %x_hbm.1, s32[4,4096]{1,0:T(4,128)} %labels_hbm.1, bf16[32,32]{1,0:T(8,128)(2,1)} %receiver_hbm.1, bf16[32,128]{1,0:T(8,128)(2,1)} %bitcast.4, bf16[32,128]{1,0:T(8,128)(2,1)} %bitcast.5, ...), custom_call_target="tpu_custom_call" | custom-call | tf_op jit(solution)/shard_map/totals/pallas_call | solution.py:264
  3.6 17.5 %all_to_all.15.got_ref = bf16[4,144,128]{2,1,0:T(8,128)(2,1)S(1)} all-to-all(bf16[4,144,128]{2,1,0:T(8,128)(2,1)S(1)} %get-tuple-element.10), channel_id=1, replica_groups=mesh['samp'=8,'part'=4,'line'=4,'recv'=4] {'recv'}, dimensions={0} | all-to-all | bytes 294912 | tf_op jit(solution)/shard_map/all_to_all | solution.py:294
  21.1 0.3 tables.1
  21.4 12.0 %all_to_all.16.refs_0_ = bf16[16,32,128]{2,1,0:T(8,128)(2,1)S(1)} all-to-all(bf16[16,32,128]{2,1,0:T(8,128)(2,1)S(1)} %get-tuple-element.13), channel_id=1, replica_groups=mesh['samp'=8,'part'=4,'line'=4,'recv'=4] {'line','part'}, dimensions={0} | all-to-all | bytes 262144 | tf_op jit(solution)/shard_map/all_to_all | solution.py:305
  33.5 0.5 %product.1 = f32[16,1,128]{2,1,0:T(1,128)S(1)} custom-call(bf16[16,32,128]{2,1,0:T(8,128)(2,1)S(1)} %all_to_all.16.refs_0_), custom_call_target="tpu_custom_call" | custom-call | tf_op jit(solution)/shard_map/product/pallas_call | solution.py:306
  34.0 11.3 %all_to_all.17.refs_0_ = f32[16,1,128]{2,1,0:T(1,128)S(1)} all-to-all(f32[16,1,128]{2,1,0:T(1,128)S(1)} %product.1), channel_id=1, replica_groups=mesh['samp'=8,'part'=4,'line'=4,'recv'=4] {'part','recv'}, dimensions={0} | all-to-all | bytes 16384 | tf_op jit(solution)/shard_map/all_to_all | solution.py:313
  45.3 1.7 %solve.1 = f32[4,32]{1,0:T(4,128)} custom-call(f32[16,1,128]{2,1,0:T(1,128)S(1)} %all_to_all.17.refs_0_, f32[32,32]{1,0:T(8,128)S(1)} %get-tuple-element.14.refs_1_), custom_call_target="tpu_custom_call" | custom-call | tf_op jit(solution)/shard_map/solve/pallas_call | solution.py:314
